TPU v7x, 32 devices: a whole 2x2x4 slice. The times are simulated.
32 devices in a mesh: rows: 4 (over z), keys: 8 (over y, x, core).
Axes of the slice: x: 2, y: 2, z: 4, core: 2. Of those that a mesh axis runs over, the one named last changes fastest.
Arguments:
- tokens: bfloat16 [2, 4, 2048, 768], P(None, 'rows', 'keys'), may hold values from -6 to 6
- prev_logits: bfloat16 [2, 4, 12, 2048, 2048], P(None, 'rows', None, 'keys'), may hold values from -6 to 6
- segments: int32 [2, 4, 2048], P(None, 'rows'), may hold values from 0 to 63, as said below
- out_cot: bfloat16 [2, 4, 2048, 768], P(None, 'rows', 'keys'), may hold values from -6 to 6
- master_mat: float32 [8, 768, 1152], P('rows', None, 'keys'), may hold values from -6 to 6
- mom1_mat: float32 [8, 768, 1152], P('rows', None, 'keys'), may hold values from -38.4 to 38.4
- mom2_mat: float32 [8, 768, 1152], P('rows', None, 'keys'), as said below
- eigen_bases: float32 [8, 768, 768], P('rows'), may hold values from -1 to 1
- master_small: float32 [8, 1152], P('rows', 'keys'), may hold values from -2 to 2
- mom1_small: float32 [8, 1152], P('rows', 'keys'), may hold values from -38.4 to 38.4
- mom2_small: float32 [8, 1152], P('rows', 'keys'), as said below
- owners: int32 [8], replicated, may hold values from 0 to 7, as said below
- step_count: int32 [1], replicated, may hold values from 2 to 20
Outputs:
- out_hidden: bfloat16 [2, 4, 2048, 768], P(None, 'rows', 'keys')
- logits: bfloat16 [2, 4, 12, 2048, 2048], P(None, 'rows', None, 'keys')
- grad_tokens: bfloat16 [2, 4, 2048, 768], P(None, 'rows', 'keys')
- grad_prev: bfloat16 [2, 4, 12, 2048, 2048], P(None, 'rows', None, 'keys')
- grad_mat: float32 [8, 768, 1152], P('rows', None, 'keys')
- new_mom1_mat: float32 [8, 768, 1152], P('rows', None, 'keys')
- new_mom2_mat: float32 [8, 768, 1152], P('rows', None, 'keys')
- new_master_mat: float32 [8, 768, 1152], P('rows', None, 'keys')
- copy_mat: bfloat16 [8, 768, 1152], P('rows', None, 'keys')
- grad_small: float32 [8, 1152], P('rows', 'keys')
- new_mom1_small: float32 [8, 1152], P('rows', 'keys')
- new_mom2_small: float32 [8, 1152], P('rows', 'keys')
- new_master_small: float32 [8, 1152], P('rows', 'keys')
- copy_small: bfloat16 [8, 1152], P('rows', 'keys')
Inputs may be any that keep to these rules, and one draw needn't show every extreme that they name: `segments`: in every packed row the ids start at 0 and rise by one at the first slot of each document; documents start only at multiples of 32 slots; a quarter of a row is wholly inside one document with probability g / 3 for rows index g, and two such quarters side by side belong to the same document; every other quarter starts a new document at its first slot and is cut at each further multiple of 32 with probability one half; the first row of the first micro-batch holds 64 documents. `owners`: A permutation. `mom2_mat`: Positive. `mom2_small`: Positive.
All inputs are finite; a program needn't handle non-finite values.
Results may differ from a plain program's by a relative error of at most 0.025.
Values may be sent and summed in bfloat16 or wider, within the bound.
A program may use at most 448 MiB of HBM per device.

v0:
```python
import jax
import jax.numpy as jnp
from jax import lax
from jax.sharding import PartitionSpec as P

MODEL_WIDTH = 768
H = 12
HD = 64
FF = 3072
BLOCK_COLUMNS = 1152
GAIN_ROW_WIDTH = 1152


EPS_NORM = 1e-06
BETA_ONE = 0.95
BETA_TWO = 0.95
EPS_ADAM = 1e-08
DECAY = 0.01
RATE_SMALL = 0.3
NEG_BIG = -1e30
HIGHEST_PREC = lax.Precision.HIGHEST


def layer_norm(value):
    mean_val = jnp.mean(value, axis=-1, keepdims=True)
    centered = value - mean_val
    inv_dev = lax.rsqrt(jnp.mean(centered * centered, axis=-1, keepdims=True) + EPS_NORM)
    return (centered * inv_dev, inv_dev)


def norm_back(grad_in, normed, inv_dev, gain):
    scaled = grad_in * gain
    return inv_dev * (
        scaled
        - jnp.mean(scaled, axis=-1, keepdims=True)
        - normed * jnp.mean(scaled * normed, axis=-1, keepdims=True)
    )


def inverse_order(owners):
    slot_index_list = jnp.arange(owners.shape[0], dtype=jnp.int32)
    matches = (owners[None, :] == slot_index_list[:, None]).astype(jnp.int32)
    return jnp.sum(matches * slot_index_list[None, :], axis=1)


def column_rates(columns):
    inner = MODEL_WIDTH ** (-0.5)
    return jnp.where(
        columns < 3 * MODEL_WIDTH,
        inner,
        jnp.where(
            columns < 4 * MODEL_WIDTH,
            4.0 * inner,
            jnp.where(columns < 4 * MODEL_WIDTH + FF, inner, FF ** (-0.5)),
        ),
    )


def contract_rows(left, right):
    return lax.dot_general(
        left, right, (((0,), (0,)), ((), ())), preferred_element_type=jnp.float32
    )


def contract_cols(left, right):
    return lax.dot_general(
        left, right, (((1,), (1,)), ((), ())), preferred_element_type=jnp.float32
    )


def unpack(gathered_mat, gathered_small, owners):
    weight_blocks = jnp.take(gathered_mat, owners, axis=0)
    packed_weights = jnp.transpose(weight_blocks, (1, 0, 2)).reshape(
        MODEL_WIDTH, 4 * MODEL_WIDTH + 2 * FF
    )
    return (packed_weights, gathered_small.reshape(8 * MODEL_WIDTH + FF).astype(jnp.float32))


def per_device(
    tokens,
    prev_logits,
    segments,
    out_cot,
    master_mat,
    mom1_mat,
    mom2_mat,
    eigen_bases,
    master_small,
    mom1_small,
    mom2_small,
    owners,
    step_count,
):
    micro, row_count, key_len, width = tokens.shape
    slot_count = prev_logits.shape[4]
    token_count = row_count * key_len
    scale = HD ** (-0.5)
    key_index = lax.axis_index("keys")
    key_start = key_index * key_len
    mat_local = master_mat.astype(jnp.bfloat16)
    small_local = master_small.astype(jnp.bfloat16).reshape(
        master_small.shape[0], 1, master_small.shape[1]
    )
    grad_mat = jnp.zeros((MODEL_WIDTH, 4 * MODEL_WIDTH + 2 * FF), jnp.float32)
    grad_small = jnp.zeros((8 * MODEL_WIDTH + FF,), jnp.float32)
    out_list = []
    logit_list = []
    token_grads = []
    prev_grads = []
    for micro_step in range(micro):
        wide_each = (
            lax.all_gather(mat_local, "keys", axis=2, tiled=True),
            lax.all_gather(small_local, "keys", axis=2, tiled=True),
        )
        full_each = (
            lax.all_gather(wide_each[0], "rows", axis=0, tiled=True),
            lax.all_gather(wide_each[1], "rows", axis=0, tiled=True),
        )
        packed_weights, params = unpack(full_each[0], full_each[1], owners)
        w_qkv = packed_weights[:, : 3 * MODEL_WIDTH]
        w_out = packed_weights[:, 3 * MODEL_WIDTH : 4 * MODEL_WIDTH]
        w_up = packed_weights[:, 4 * MODEL_WIDTH : 4 * MODEL_WIDTH + FF]
        w_down = packed_weights[:, 4 * MODEL_WIDTH + FF :]
        bias_q = params[:MODEL_WIDTH]
        bias_v = params[MODEL_WIDTH : 2 * MODEL_WIDTH]
        bias_o = params[2 * MODEL_WIDTH : 3 * MODEL_WIDTH]
        gain_one = params[3 * MODEL_WIDTH : 4 * MODEL_WIDTH]
        shift_one = params[4 * MODEL_WIDTH : 5 * MODEL_WIDTH]
        bias_up = params[5 * MODEL_WIDTH : 5 * MODEL_WIDTH + FF]
        bias_down = params[5 * MODEL_WIDTH + FF : 6 * MODEL_WIDTH + FF]
        gain_two = params[6 * MODEL_WIDTH + FF : 7 * MODEL_WIDTH + FF]
        shift_two = params[7 * MODEL_WIDTH + FF :]
        x_rows = tokens[micro_step].reshape(token_count, MODEL_WIDTH)
        projected = jnp.dot(x_rows, w_qkv, preferred_element_type=jnp.float32)
        queries_own = (
            (projected[:, :MODEL_WIDTH] + bias_q)
            .astype(jnp.bfloat16)
            .reshape(row_count, key_len, MODEL_WIDTH)
        )
        keys_own = (
            projected[:, MODEL_WIDTH : 2 * MODEL_WIDTH]
            .astype(jnp.bfloat16)
            .reshape(row_count, key_len, H, HD)
        )
        values_own = (
            (projected[:, 2 * MODEL_WIDTH :] + bias_v)
            .astype(jnp.bfloat16)
            .reshape(row_count, key_len, H, HD)
        )
        queries_all = lax.all_gather(queries_own, "keys", axis=1, tiled=True).reshape(
            row_count, slot_count, H, HD
        )
        seg_rows = segments[micro_step]
        seg_keys = lax.dynamic_slice_in_dim(seg_rows, key_start, key_len, 1)
        allowed = (seg_keys[:, :, None] == seg_rows[:, None, :])[:, None, :, :]
        prev_rows = prev_logits[micro_step].astype(jnp.float32)
        raw_scores = (
            jnp.einsum("rjhd,rihd->rhji", keys_own, queries_all, preferred_element_type=jnp.float32)
            * scale
            + prev_rows
        )
        logit_list.append(raw_scores.astype(jnp.bfloat16))
        local_top = jnp.max(jnp.where(allowed, raw_scores, NEG_BIG), axis=2)
        row_top = lax.pmax(local_top.astype(jnp.bfloat16), "keys").astype(local_top.dtype)
        row_total = lax.psum(
            jnp.sum(jnp.where(allowed, jnp.exp(raw_scores - row_top[:, :, None, :]), 0.0), axis=2),
            "keys",
        )
        soft_now = (
            jnp.where(allowed, jnp.exp(raw_scores - row_top[:, :, None, :]), 0.0)
            / row_total[:, :, None, :]
        )
        soft_low = soft_now.astype(jnp.bfloat16)
        attended = lax.psum_scatter(
            jnp.einsum(
                "rhji,rjhd->irhd", soft_low, values_own, preferred_element_type=jnp.float32
            ).reshape(key_len * lax.axis_size("keys"), row_count, MODEL_WIDTH),
            "keys",
            scatter_dimension=0,
            tiled=True,
        )
        att_low = (
            jnp.transpose(attended, (1, 0, 2))
            .reshape(token_count, MODEL_WIDTH)
            .astype(jnp.bfloat16)
        )
        branch = jnp.dot(att_low, w_out, preferred_element_type=jnp.float32) + bias_o
        normed_one, inv_one = layer_norm(x_rows.astype(jnp.float32) + branch)
        mid_act = normed_one * gain_one + shift_one
        mid_low = mid_act.astype(jnp.bfloat16)
        pre_act = jnp.dot(mid_low, w_up, preferred_element_type=jnp.float32) + bias_up
        hidden = jax.nn.gelu(pre_act, approximate=False).astype(jnp.bfloat16)
        ffn_out = contract_cols(hidden, w_down) + bias_down
        normed_two, inv_two = layer_norm(mid_act + ffn_out)
        out_list.append(
            (normed_two * gain_two + shift_two)
            .astype(jnp.bfloat16)
            .reshape(row_count, key_len, MODEL_WIDTH)
        )
        grad_out = out_cot[micro_step].reshape(token_count, MODEL_WIDTH).astype(jnp.float32)
        grad_sum_two = norm_back(grad_out, normed_two, inv_two, gain_two)
        d_gain_two = jnp.sum(grad_out * normed_two, axis=0)
        d_shift_two = jnp.sum(grad_out, axis=0)
        grad_ffn = grad_sum_two.astype(jnp.bfloat16)
        d_bias_down = jnp.sum(grad_ffn.astype(jnp.float32), axis=0)
        d_down = contract_rows(grad_ffn, hidden)
        grad_hidden = jnp.dot(grad_ffn, w_down, preferred_element_type=jnp.float32)
        gelu_value, gelu_back = jax.vjp(
            lambda value: jax.nn.gelu(value, approximate=False), pre_act
        )
        grad_pre = gelu_back(grad_hidden)[0].astype(jnp.bfloat16)
        d_bias_up = jnp.sum(grad_pre.astype(jnp.float32), axis=0)
        d_up = contract_rows(mid_low, grad_pre)
        grad_mid = grad_sum_two + contract_cols(grad_pre, w_up)
        grad_one = norm_back(grad_mid, normed_one, inv_one, gain_one)
        d_gain_one = jnp.sum(grad_mid * normed_one, axis=0)
        d_shift_one = jnp.sum(grad_mid, axis=0)
        grad_branch = grad_one.astype(jnp.bfloat16)
        d_bias_o = jnp.sum(grad_branch.astype(jnp.float32), axis=0)
        d_out = contract_rows(att_low, grad_branch)
        grad_att = (
            contract_cols(grad_branch, w_out)
            .astype(jnp.bfloat16)
            .reshape(row_count, key_len, MODEL_WIDTH)
        )
        grad_att_all = lax.all_gather(grad_att, "keys", axis=1, tiled=True).reshape(
            row_count, slot_count, H, HD
        )
        raw_again = (
            jnp.einsum("rjhd,rihd->rhji", keys_own, queries_all, preferred_element_type=jnp.float32)
            * scale
            + prev_rows
        )
        soft_again = (
            jnp.where(allowed, jnp.exp(raw_again - row_top[:, :, None, :]), 0.0)
            / row_total[:, :, None, :]
        )
        soft_again_low = soft_again.astype(jnp.bfloat16)
        grad_soft = jnp.einsum(
            "rihd,rjhd->rhji", grad_att_all, values_own, preferred_element_type=jnp.float32
        )
        grad_value = jnp.einsum(
            "rhji,rihd->rjhd", soft_again_low, grad_att_all, preferred_element_type=jnp.float32
        ).astype(jnp.bfloat16)
        row_dots = lax.psum(jnp.sum(soft_again * grad_soft, axis=2), "keys")
        grad_raw = (soft_again * (grad_soft - row_dots[:, :, None, :])).astype(jnp.bfloat16)
        prev_grads.append(grad_raw)
        grad_key = (
            jnp.einsum("rhji,rihd->rjhd", grad_raw, queries_all, preferred_element_type=jnp.float32)
            * scale
        ).astype(jnp.bfloat16)
        grad_query_sum = lax.psum_scatter(
            (
                jnp.einsum(
                    "rhji,rjhd->irhd", grad_raw, keys_own, preferred_element_type=jnp.float32
                ).reshape(lax.axis_size("keys") * key_len, row_count, MODEL_WIDTH)
                * scale
            ).astype(jnp.bfloat16),
            "keys",
            scatter_dimension=0,
            tiled=True,
        ).astype(jnp.float32)
        grad_query = (
            jnp.transpose(grad_query_sum, (1, 0, 2))
            .reshape(token_count, MODEL_WIDTH)
            .astype(jnp.bfloat16)
        )
        grad_proj = jnp.concatenate(
            [
                grad_query,
                grad_key.reshape(token_count, MODEL_WIDTH),
                grad_value.reshape(token_count, MODEL_WIDTH),
            ],
            axis=1,
        )
        d_qkv = contract_rows(x_rows, grad_proj)
        d_bias_q = jnp.sum(grad_query.astype(jnp.float32), axis=0)
        d_bias_v = jnp.sum(grad_value.reshape(token_count, MODEL_WIDTH).astype(jnp.float32), axis=0)
        grad_x = grad_one + contract_cols(grad_proj, w_qkv)
        token_grads.append(grad_x.astype(jnp.bfloat16).reshape(row_count, key_len, MODEL_WIDTH))
        grad_mat = grad_mat + jnp.concatenate([d_qkv, d_out, d_up, d_down], axis=1)
        grad_small = grad_small + jnp.concatenate(
            [
                d_bias_q,
                d_bias_v,
                d_bias_o,
                d_gain_one,
                d_shift_one,
                d_bias_up,
                d_bias_down,
                d_gain_two,
                d_shift_two,
            ]
        )
    inverse = inverse_order(owners)
    slot_total = owners.shape[0]
    weight_blocks = jnp.transpose(
        grad_mat.reshape(MODEL_WIDTH, slot_total, BLOCK_COLUMNS), (1, 0, 2)
    )
    slot_grads = jnp.take(weight_blocks, inverse, axis=0)
    small_grads = grad_small.reshape(slot_total, 1, GAIN_ROW_WIDTH)
    part_mat, part_small = (
        lax.psum_scatter(
            slot_grads.astype(jnp.bfloat16), "keys", scatter_dimension=2, tiled=True
        ).astype(jnp.float32),
        lax.psum_scatter(
            small_grads.astype(jnp.bfloat16), "keys", scatter_dimension=2, tiled=True
        ).astype(jnp.float32),
    )
    mine_mat, mine_small = (
        lax.psum_scatter(
            part_mat.astype(jnp.bfloat16), "rows", scatter_dimension=0, tiled=True
        ).astype(jnp.float32),
        lax.psum_scatter(
            part_small.astype(jnp.bfloat16), "rows", scatter_dimension=0, tiled=True
        ).astype(jnp.float32),
    )
    mine_small = mine_small.reshape(master_small.shape)
    steps_done = step_count[0].astype(jnp.float32)
    fix_one = 1.0 - jnp.power(jnp.asarray(BETA_ONE, jnp.float32), steps_done)
    fix_two = 1.0 - jnp.power(jnp.asarray(BETA_TWO, jnp.float32), steps_done)
    rotated = jnp.einsum("sed,sec->sdc", eigen_bases, mine_mat, precision=HIGHEST_PREC)
    new_one = BETA_ONE * mom1_mat + (1.0 - BETA_ONE) * rotated
    new_two = BETA_TWO * mom2_mat + (1.0 - BETA_TWO) * rotated * rotated
    direction = new_one / fix_one / (jnp.sqrt(new_two / fix_two) + EPS_ADAM)
    back_rot = jnp.einsum("sdk,skc->sdc", eigen_bases, direction, precision=HIGHEST_PREC)
    slots_here = master_mat.shape[0]
    cols_here = master_mat.shape[2]
    slot_index_list = lax.axis_index("rows") * slots_here + jnp.arange(slots_here, dtype=jnp.int32)
    block_ids = jnp.take(inverse, slot_index_list)
    columns = (
        block_ids[:, None] * (cols_here * lax.axis_size("keys"))
        + key_index * cols_here
        + jnp.arange(cols_here, dtype=jnp.int32)[None, :]
    )
    rates = column_rates(columns)[:, None, :]
    new_master = master_mat - rates * (back_rot + DECAY * master_mat)
    small_one = BETA_ONE * mom1_small + (1.0 - BETA_ONE) * mine_small
    small_two = BETA_TWO * mom2_small + (1.0 - BETA_TWO) * mine_small * mine_small
    new_small = master_small - RATE_SMALL * (small_one / fix_one) / (
        jnp.sqrt(small_two / fix_two) + EPS_ADAM
    )
    return (
        jnp.stack(out_list),
        jnp.stack(logit_list),
        jnp.stack(token_grads),
        jnp.stack(prev_grads),
        mine_mat,
        new_one,
        new_two,
        new_master,
        new_master.astype(jnp.bfloat16),
        mine_small,
        small_one,
        small_two,
        new_small,
        new_small.astype(jnp.bfloat16),
    )


def solution(mesh):
    placed = (
        P(None, "rows", "keys", None),
        P(None, "rows", None, "keys", None),
        P(None, "rows", None),
        P(None, "rows", "keys", None),
        P("rows", None, "keys"),
        P("rows", None, "keys"),
        P("rows", None, "keys"),
        P("rows", None, None),
        P("rows", "keys"),
        P("rows", "keys"),
        P("rows", "keys"),
        P(),
        P(),
    )
    return jax.shard_map(
        per_device,
        mesh=mesh,
        in_specs=placed,
        out_specs=(
            P(None, "rows", "keys", None),
            P(None, "rows", None, "keys", None),
            P(None, "rows", "keys", None),
            P(None, "rows", None, "keys", None),
            P("rows", None, "keys"),
            P("rows", None, "keys"),
            P("rows", None, "keys"),
            P("rows", None, "keys"),
            P("rows", None, "keys"),
            P("rows", "keys"),
            P("rows", "keys"),
            P("rows", "keys"),
            P("rows", "keys"),
            P("rows", "keys"),
        ),
        check_vma=False,
    )
```

profile of v0, /device:TPU:8, one launch (start us, length us, event | category | flops | bytes accessed | tf_op | source)
XLA Modules:
  0.0 1287.7 jit_solution(16767689632710605505)
XLA Ops:
  9.9 35.7 %all-gather.15.cloned.1.call-done = bf16[2,768,1152]{1,0,2:T(2,128)(2,1)} async-done(((bf16[2,768,144]{1,0,2:T(2,128)(2,1)}), bf16[2,768,1152]{1,0,2:T(2,128)(2,1)}) %all-gather.15.cloned.1.call-update) | async-done | bytes 3538960 | tf_op jit(solution)/shard_map/all_gather | solution.py:112
  65.6 16.0 %all-gather.7 = bf16[4,2,1152]{2,1,0:T(2,128)(2,1)S(1)} all-gather(bf16[1,2,1152]{2,1,0:T(2,128)(2,1)S(1)} %bitcast.299), channel_id=3, replica_groups=mesh['rows'=4,'keys'=8] {'rows'}, dimensions={0}, use_global_device_ids=true | all-gather | bytes 23040 | tf_op jit(solution)/shard_map/all_gather | solution.py:117
  82.2 215.1 %all-gather.17.cloned.1.call-done = bf16[8,768,1152]{2,1,0:T(8,128)(2,1)} async-done(((bf16[2,768,1152]{2,1,0:T(8,128)(2,1)}), bf16[8,768,1152]{2,1,0:T(8,128)(2,1)}) %all-gather.17.cloned.1.call-update) | async-done | bytes 14155792 | tf_op jit(solution)/shard_map/all_gather | solution.py:116
  297.3 12.5 gather_fusion.2
  309.8 13.1 %select_bitcast_fusion = bf16[768,8,1152]{2,0,1:T(8,128)(2,1)} fusion(bf16[8,768,1152]{2,1,0:T(8,128)(2,1)} %gather_fusion.2, pred[8]{0:T(512)(128)(4,1)S(1)} %compare_and_fusion), kind=kLoop, calls=%fused_computation.22 | loop fusion | flops 7077888 | bytes 28311560 | tf_op jit(solution)/shard_map/transpose | solution.py:73
  322.9 18.7 %copy.97 = bf16[768,8,1152]{0,2,1:T(8,128)(2,1)} copy(bf16[768,8,1152]{2,0,1:T(8,128)(2,1)} %select_bitcast_fusion) | data formatting | bytes 28311552 | tf_op jit(solution)/shard_map/transpose | solution.py:73
  355.8 29.8 %all-gather.21.cloned.1.call-done = bf16[2048,768]{0,1:T(8,128)(2,1)} async-done(((bf16[256,768]{0,1:T(8,128)(2,1)}), bf16[2048,768]{0,1:T(8,128)(2,1)}) %all-gather.21.cloned.1.call-update) | async-done | bytes 3145744 | tf_op jit(solution)/shard_map/all_gather | solution.py:150
  385.6 17.0 %select_reduce_fusion = (bf16[12,2048]{1,0:T(8,128)(2,1)}, f32[12,256,2048]{2,1,0:T(8,128)}) fusion(pred[256,2048]{1,0:T(8,128)(4,1)S(1)} %broadcast_compare_fusion, bf16[2,1,12,256,2048]{4,3,2,1,0:T(8,128)(2,1)} %param.16, bf16[256,12,64]{0,2,1:T(8,128)(2,1)S(1)} %bitcast.276, bf16[2048,12,64]{0,2,1:T(8,128)(2,1)} %bitcast.271), kind=kOutput, calls=%fused_computation.15 | convolution fusion | flops 836739072 | bytes 41861120 | tf_op jit(solution)/shard_map/rjhd,rihd->rhji/dot_general | solution.py:158
  402.6 18.1 %all-gather.19.cloned.1.call-done = bf16[2048,768]{0,1:T(8,128)(2,1)} async-done(((bf16[256,768]{0,1:T(8,128)(2,1)}), bf16[2048,768]{0,1:T(8,128)(2,1)}) %all-gather.19.cloned.1.call-update) | async-done | bytes 3145744 | tf_op jit(solution)/shard_map/all_gather | solution.py:150
  420.7 17.0 %select_reduce_fusion.1 = (bf16[12,2048]{1,0:T(8,128)(2,1)}, f32[12,256,2048]{2,1,0:T(8,128)}) fusion(pred[256,2048]{1,0:T(8,128)(4,1)S(1)} %broadcast_compare_fusion.1, bf16[2,1,12,256,2048]{4,3,2,1,0:T(8,128)(2,1)} %param.16, bf16[256,12,64]{0,2,1:T(8,128)(2,1)S(1)} %bitcast.278, bf16[2048,12,64]{0,2,1:T(8,128)(2,1)} %bitcast.273), kind=kOutput, calls=%fused_computation.17 | convolution fusion | flops 836739072 | bytes 41861120 | tf_op jit(solution)/shard_map/rjhd,rihd->rhji/dot_general | solution.py:158
  437.8 53.2 %all-reduce.12.cloned.1.call-done = (bf16[12,2048]{1,0:T(8,128)(2,1)}, bf16[12,2048]{1,0:T(8,128)(2,1)}) async-done(((bf16[12,2048]{1,0:T(8,128)(2,1)}, bf16[12,2048]{1,0:T(8,128)(2,1)}), (bf16[12,2048]{1,0:T(8,128)(2,1)}, bf16[12,2048]{1,0:T(8,128)(2,1)})) %all-reduce.12.cloned.1.call-update) | async-done | bytes 98320 | tf_op jit(solution)/shard_map/pmax | solution.py:164
  492.8 11.7 fusion.1
  514.0 52.9 %all-reduce.10.cloned.1.call-done = (f32[12,2048]{1,0:T(8,128)}, f32[12,2048]{1,0:T(8,128)}) async-done(((f32[12,2048]{1,0:T(8,128)}, f32[12,2048]{1,0:T(8,128)}), (f32[12,2048]{1,0:T(8,128)}, f32[12,2048]{1,0:T(8,128)})) %all-reduce.10.cloned.1.call-update) | async-done | bytes 196624 | tf_op jit(solution)/shard_map/psum | solution.py:165
  566.9 13.1 %fusion.6 = f32[12,64,2048]{2,1,0:T(8,128)} fusion(bf16[256,12,64]{0,2,1:T(8,128)(2,1)S(1)} %bitcast.293, f32[12,256,2048]{2,1,0:T(8,128)} %get-tuple-element.144, f32[12,2048]{1,0:T(8,128)} %get-tuple-element.91, f32[12,2048]{1,0:T(8,128)S(1)} %sub.162, pred[256,2048]{1,0:T(8,128)(4,1)S(1)} %broadcast_compare_fusion), kind=kOutput, calls=%fused_computation.29 | convolution fusion | flops 830472192 | bytes 32571392 | tf_op jit(solution)/shard_map/rhji,rjhd->irhd/dot_general | solution.py:175
  581.0 15.9 %fusion.10 = f32[12,64,2048]{2,1,0:T(8,128)} fusion(bf16[256,12,64]{0,2,1:T(8,128)(2,1)S(1)} %bitcast.295, f32[12,256,2048]{2,1,0:T(8,128)} %get-tuple-element.146, f32[12,2048]{1,0:T(8,128)S(1)} %copy-done.60, f32[12,2048]{1,0:T(8,128)S(1)} %sub.154, pred[256,2048]{1,0:T(8,128)(4,1)S(1)} %broadcast_compare_fusion.1), kind=kOutput, calls=%fused_computation.33 | convolution fusion | flops 830472192 | bytes 32571392 | tf_op jit(solution)/shard_map/rhji,rjhd->irhd/dot_general | solution.py:175
  597.4 43.9 %reduce-scatter.13.cloned.1.call-done = f32[256,1,768]{0,2,1:T(8,128)} async-done(((f32[2048,1,768]{0,2,1:T(8,128)}), f32[256,1,768]{0,2,1:T(8,128)}) %reduce-scatter.13.cloned.1.call-update) | async-done | bytes 786448 | tf_op jit(solution)/shard_map/reduce_scatter | solution.py:174
  660.5 46.4 %reduce-scatter.11.cloned.1.call-done = f32[256,1,768]{0,2,1:T(8,128)} async-done(((f32[2048,1,768]{0,2,1:T(8,128)}), f32[256,1,768]{0,2,1:T(8,128)}) %reduce-scatter.11.cloned.1.call-update) | async-done | bytes 786448 | tf_op jit(solution)/shard_map/reduce_scatter | solution.py:174
  775.8 20.3 %multiply_reduce_fusion.1 = (f32[12,2048]{1,0:T(8,128)}, f32[12,256,2048]{2,1,0:T(8,128)}) fusion(f32[12,2048]{1,0:T(8,128)S(1)} %copy-done.60, f32[12,256,2048]{2,1,0:T(8,128)} %get-tuple-element.146, f32[12,2048]{1,0:T(8,128)S(1)} %sub.154, pred[256,2048]{1,0:T(8,128)(4,1)S(1)} %copy-done.13, bf16[256,12,64]{0,2,1:T(8,128)(2,1)S(1)} %bitcast.296, ...), kind=kOutput, calls=%fused_computation.13 | convolution fusion | flops 836739072 | bytes 54689792 | tf_op jit(solution)/shard_map/rihd,rjhd->rhji/dot_general | solution.py:239
  809.9 19.9 %multiply_reduce_fusion = (f32[12,2048]{1,0:T(8,128)}, f32[12,256,2048]{2,1,0:T(8,128)}) fusion(f32[12,2048]{1,0:T(8,128)S(1)} %copy-done.61, f32[12,256,2048]{2,1,0:T(8,128)} %get-tuple-element.144, f32[12,2048]{1,0:T(8,128)S(1)} %copy-done.51, pred[256,2048]{1,0:T(8,128)(4,1)S(1)} %copy-done.15, bf16[256,12,64]{0,2,1:T(8,128)(2,1)S(1)} %bitcast.294, ...), kind=kOutput, calls=%fused_computation.11 | convolution fusion | flops 836739072 | bytes 54689792 | tf_op jit(solution)/shard_map/rihd,rjhd->rhji/dot_general | solution.py:239
  831.8 51.8 %all-reduce.8.cloned.1.call-done = (f32[12,2048]{1,0:T(8,128)}, f32[12,2048]{1,0:T(8,128)}) async-done(((f32[12,2048]{1,0:T(8,128)}, f32[12,2048]{1,0:T(8,128)}), (f32[12,2048]{1,0:T(8,128)}, f32[12,2048]{1,0:T(8,128)})) %all-reduce.8.cloned.1.call-update) | async-done | bytes 196624 | tf_op jit(solution)/shard_map/psum | solution.py:245
  883.7 30.0 %multiply_convert_fusion.1 = (bf16[12,256,2048]{2,1,0:T(8,128)(2,1)S(1)}, bf16[1,1,12,256,2048]{4,3,2,1,0:T(8,128)(2,1)}) fusion(f32[12,256,2048]{2,1,0:T(8,128)} %get-tuple-element.162, f32[12,2048]{1,0:T(8,128)} %get-tuple-element.90, f32[12,2048]{1,0:T(8,128)S(1)} %copy-done.60, f32[12,256,2048]{2,1,0:T(8,128)} %get-tuple-element.146, ...), kind=kLoop, calls=%fused_computation.12 | loop fusion | flops 44040192 | bytes 76316672 | tf_op jit(solution)/shard_map/convert_element_type | solution.py:246
  919.3 14.0 %convert_reduce_fusion.6 = (f32[12,64]{1,0:T(8,128)S(1)}, bf16[12,64,256]{2,1,0:T(8,128)(2,1)}) fusion(bf16[2048,12,64]{0,2,1:T(8,128)(2,1)} %bitcast.270, f32[12,2048]{1,0:T(8,128)S(1)} %copy-done.61, f32[12,256,2048]{2,1,0:T(8,128)} %get-tuple-element.144, f32[12,2048]{1,0:T(8,128)S(1)} %copy-done.51, pred[256,2048]{1,0:T(8,128)(4,1)S(1)} %copy-done.15), kind=kOutput, calls=%fused_computation.176 | convolution fusion | flops 831061248 | bytes 29428736 | tf_op jit(solution)/shard_map/rhji,rihd->rjhd/dot_general | solution.py:242
  933.3 30.2 %multiply_convert_fusion = (bf16[12,256,2048]{2,1,0:T(8,128)(2,1)S(1)}, bf16[1,1,12,256,2048]{4,3,2,1,0:T(8,128)(2,1)}) fusion(f32[12,256,2048]{2,1,0:T(8,128)} %get-tuple-element.160, f32[12,2048]{1,0:T(8,128)S(1)} %copy-done.62, f32[12,2048]{1,0:T(8,128)S(1)} %copy-done.61, f32[12,256,2048]{2,1,0:T(8,128)} %get-tuple-element.144, ...), kind=kLoop, calls=%fused_computation.10 | loop fusion | flops 44040192 | bytes 76316672 | tf_op jit(solution)/shard_map/convert_element_type | solution.py:246
  969.0 13.7 %convert_reduce_fusion.10 = (f32[12,64]{1,0:T(8,128)S(1)}, bf16[12,64,256]{2,1,0:T(8,128)(2,1)S(1)}) fusion(bf16[2048,12,64]{0,2,1:T(8,128)(2,1)} %bitcast.268, f32[12,2048]{1,0:T(8,128)S(1)} %copy-done.60, f32[12,256,2048]{2,1,0:T(8,128)} %get-tuple-element.146, f32[12,2048]{1,0:T(8,128)S(1)} %sub.154, pred[256,2048]{1,0:T(8,128)(4,1)S(1)} %copy-done.13), kind=kOutput, calls=%fused_computation.181 | convolution fusion | flops 831061248 | bytes 29428736 | tf_op jit(solution)/shard_map/rhji,rihd->rjhd/dot_general | solution.py:242
  1020.2 17.0 %maximum_add_fusion = bf16[768,9216]{1,0:T(8,128)(2,1)S(1)} fusion(f32[768,3072]{1,0:T(8,128)} %fusion.169, f32[768,3072]{1,0:T(8,128)} %fusion.175, f32[768,768]{1,0:T(8,128)} %fusion.140, f32[768,2304]{1,0:T(8,128)} %copy.101, f32[768,3072]{1,0:T(8,128)} %fusion.164, f32[768,3072]{1,0:T(8,128)} %fusion.172, f32[768,768]{1,0:T(8,128)S(1)} %copy-done.5, ...), kind=kLoop, calls=%fused_computation.4 | loop fusion | flops 56623104 | bytes 70778880 | tf_op jit(solution)/shard_map/add | solution.py:281
  1043.0 12.8 gather_fusion
  1055.9 13.9 %select_convert_fusion = bf16[8,768,1152]{2,1,0:T(8,128)(2,1)} fusion(bf16[8,768,1152]{2,1,0:T(8,128)(2,1)} %gather_fusion, pred[8]{0:T(512)(128)(4,1)S(1)} %copy-done.83), kind=kLoop, calls=%fused_computation.5 | loop fusion | flops 7077888 | bytes 28311560 | tf_op jit(solution)/shard_map/convert_element_type | solution.py:304
  1069.8 19.7 %copy.106 = bf16[8,768,1152]{1,0,2:T(8,128)(2,1)} copy(bf16[8,768,1152]{2,1,0:T(8,128)(2,1)} %select_convert_fusion) | data formatting | bytes 28311552 | tf_op jit(solution)/shard_map/convert_element_type | solution.py:304
  1096.2 94.3 %reduce-scatter.19.cloned.1.call-done = bf16[8,768,144]{1,0,2:T(8,128)(2,1)} async-done(((bf16[8,768,1152]{1,0,2:T(8,128)(2,1)}), bf16[8,768,144]{1,0,2:T(8,128)(2,1)}) %reduce-scatter.19.cloned.1.call-update) | async-done | bytes 1769488 | tf_op jit(solution)/shard_map/reduce_scatter | solution.py:303
  1193.6 25.2 %pad_maximum_fusion.1 = bf16[2,1,12,256,2048]{4,3,2,1,0:T(8,128)(2,1)} fusion(bf16[1,1,12,256,2048]{4,3,2,1,0:T(8,128)(2,1)} %bitcast.236, bf16[1,1,12,256,2048]{4,3,2,1,0:T(8,128)(2,1)} %bitcast.235), kind=kLoop, calls=%fused_computation.7 | loop fusion | flops 12582912 | bytes 50331648 | tf_op jit(solution)/shard_map/stack | solution.py:347
  1218.9 11.8 pad_maximum_fusion
  1244.9 21.8 %reduce-scatter.21.cloned.1.call-done = bf16[2,768,144]{1,2,0:T(8,128)(2,1)} async-done(((bf16[8,768,144]{1,2,0:T(8,128)(2,1)}), bf16[2,768,144]{1,2,0:T(8,128)(2,1)}) %reduce-scatter.21.cloned.1.call-update) | async-done | bytes 442384 | tf_op jit(solution)/shard_map/reduce_scatter | solution.py:311
  (373 shorter events, 244.0 us)
Async XLA Ops:
  7.2 38.5 %all-gather.15.cloned.1.call-start = ((), (), s32[]{:S(2)}) async-start(), calls=%async_computation.7 | async-start | bytes 3981312 | tf_op jit(solution)/shard_map/all_gather | solution.py:112
  9.9 287.5 %all-gather.17.cloned.1.call-start = ((), (), s32[]{:S(2)}) async-start(), calls=%async_computation.8 | async-start | bytes 17694720 | tf_op jit(solution)/shard_map/all_gather | solution.py:116
  56.0 25.6 %copy-start.84 = (s32[8]{0:T(128)S(1)}, s32[8]{0:T(128)}, u32[]{:S(2)}) copy-start(s32[8]{0:T(128)} %param.26) | copy-start | bytes 100
  56.0 329.6 %all-gather.21.cloned.1.call-start = ((), (), s32[]{:S(2)}) async-start(), calls=%async_computation.16 | async-start | bytes 3538944 | tf_op jit(solution)/shard_map/all_gather | solution.py:150
  351.5 215.4 %copy-start.56 = (bf16[256,768]{0,1:T(8,128)(2,1)}, bf16[256,768]{0,1:T(8,128)(2,1)S(1)}, u32[]{:S(2)}) copy-start(bf16[256,768]{0,1:T(8,128)(2,1)S(1)} %get-tuple-element.119) | copy-start | bytes 1179652
  351.5 69.2 %all-gather.19.cloned.1.call-start = ((), (), s32[]{:S(2)}) async-start(), calls=%async_computation.15 | async-start | bytes 3538944 | tf_op jit(solution)/shard_map/all_gather | solution.py:150
  352.1 139.0 %all-reduce.12.cloned.1.call-start = ((), (), s32[]{:S(2)}) async-start(), calls=%async_computation.22 | async-start | bytes 262144 | tf_op jit(solution)/shard_map/pmax | solution.py:164
  352.7 214.2 %copy-start.14 = (pred[256,2048]{1,0:T(8,128)(4,1)}, pred[256,2048]{1,0:T(8,128)(4,1)S(1)}, u32[]{:S(2)}) copy-start(pred[256,2048]{1,0:T(8,128)(4,1)S(1)} %broadcast_compare_fusion) | copy-start | bytes 1572868
  353.1 227.0 %copy-start.12 = (pred[256,2048]{1,0:T(8,128)(4,1)}, pred[256,2048]{1,0:T(8,128)(4,1)S(1)}, u32[]{:S(2)}) copy-start(pred[256,2048]{1,0:T(8,128)(4,1)S(1)} %broadcast_compare_fusion.1) | copy-start | bytes 1572868
  354.5 48.1 %copy-start.30 = (bf16[256,768]{0,1:T(8,128)(2,1)}, bf16[256,768]{0,1:T(8,128)(2,1)S(1)}, u32[]{:S(2)}) copy-start(bf16[256,768]{0,1:T(8,128)(2,1)S(1)} %slice.252) | copy-start | bytes 1179652
  355.8 64.9 %copy-start.32 = (bf16[256,768]{0,1:T(8,128)(2,1)}, bf16[256,768]{0,1:T(8,128)(2,1)S(1)}, u32[]{:S(2)}) copy-start(bf16[256,768]{0,1:T(8,128)(2,1)S(1)} %slice.253) | copy-start | bytes 1179652
  437.8 129.1 %all-reduce.10.cloned.1.call-start = ((), (), s32[]{:S(2)}) async-start(), calls=%async_computation.21 | async-start | bytes 524288 | tf_op jit(solution)/shard_map/psum | solution.py:165
  492.7 74.2 %copy-start.50 = (f32[12,2048]{1,0:T(8,128)}, f32[12,2048]{1,0:T(8,128)S(1)}, u32[]{:S(2)}) copy-start(f32[12,2048]{1,0:T(8,128)S(1)} %sub.162) | copy-start | bytes 294916
  513.8 127.6 %reduce-scatter.13.cloned.1.call-start = ((), (), s32[]{:S(2)}) async-start(), calls=%async_computation.10 | async-start | bytes 7077888 | tf_op jit(solution)/shard_map/reduce_scatter | solution.py:174
  580.0 126.8 %reduce-scatter.11.cloned.1.call-start = ((), (), s32[]{:S(2)}) async-start(), calls=%async_computation.9 | async-start | bytes 7077888 | tf_op jit(solution)/shard_map/reduce_scatter | solution.py:174
  597.0 174.1 %all-gather.23.cloned.1.call-start = ((), (), s32[]{:S(2)}) async-start(), calls=%async_computation.17 | async-start | bytes 3538944 | tf_op jit(solution)/shard_map/all_gather | solution.py:226
  655.1 64.3 %slice-start.6 = ((s8[14155776]{0:T(1024)(128)(4,1)}), s8[1572864]{0:T(1024)(128)(4,1)S(1)}, s32[]{:S(2)}) async-start(s8[14155776]{0:T(1024)(128)(4,1)} %bitcast.251), calls=%async_computation.29 | async-start | bytes 3145728
  737.3 92.6 %copy-start.25 = (f32[256,768]{1,0:T(8,128)}, f32[256,768]{1,0:T(8,128)S(1)}, u32[]{:S(2)}) copy-start(f32[256,768]{1,0:T(8,128)S(1)} %get-tuple-element.107) | copy-start | bytes 2359300
  738.6 66.5 %all-gather.25.cloned.1.call-start = ((), (), s32[]{:S(2)}) async-start(), calls=%async_computation.18 | async-start | bytes 3538944 | tf_op jit(solution)/shard_map/all_gather | solution.py:226
  751.2 132.4 %all-reduce.8.cloned.1.call-start = ((), (), s32[]{:S(2)}) async-start(), calls=%async_computation.20 | async-start | bytes 524288 | tf_op jit(solution)/shard_map/psum | solution.py:245
  829.9 170.2 %reduce-scatter.15.cloned.1.call-start = ((), (), s32[]{:S(2)}) async-start(), calls=%async_computation.11 | async-start | bytes 3538944 | tf_op jit(solution)/shard_map/reduce_scatter | solution.py:252
  883.6 30.0 %copy-start.33 = (bf16[256,768]{0,1:T(8,128)(2,1)S(1)}, bf16[256,768]{0,1:T(8,128)(2,1)}, u32[]{:S(2)}) copy-start(bf16[256,768]{0,1:T(8,128)(2,1)} %copy-done.32) | copy-start | bytes 1179652
  919.3 95.6 %reduce-scatter.17.cloned.1.call-start = ((), (), s32[]{:S(2)}) async-start(), calls=%async_computation.12 | async-start | bytes 3538944 | tf_op jit(solution)/shard_map/reduce_scatter | solution.py:252
  933.3 30.2 %copy-start.31 = (bf16[256,768]{0,1:T(8,128)(2,1)S(1)}, bf16[256,768]{0,1:T(8,128)(2,1)}, u32[]{:S(2)}) copy-start(bf16[256,768]{0,1:T(8,128)(2,1)} %copy-done.30) | copy-start | bytes 1179652
  968.9 221.6 %reduce-scatter.19.cloned.1.call-start = ((), (), s32[]{:S(2)}) async-start(), calls=%async_computation.13 | async-start | bytes 15925248 | tf_op jit(solution)/shard_map/reduce_scatter | solution.py:303
  1089.7 144.4 %reduce-scatter.23.cloned.1.call-start = ((), (), s32[]{:S(2)}) async-start(), calls=%async_computation.19 | async-start | bytes 331776
  1095.2 171.4 %reduce-scatter.21.cloned.1.call-start = ((), (), s32[]{:S(2)}) async-start(), calls=%async_computation.14 | async-start | bytes 2211840 | tf_op jit(solution)/shard_map/reduce_scatter | solution.py:311
  1193.6 25.2 %slice-start = ((s8[12582912]{0:T(1024)(128)(4,1)}), s8[4194304]{0:T(1024)(128)(4,1)S(1)}, s32[]{:S(2)}) async-start(s8[12582912]{0:T(1024)(128)(4,1)} %bitcast.239), calls=%async_computation.23 | async-start | bytes 8388608
  1193.6 37.1 %slice-start.10 = ((s8[14155776]{0:T(1024)(128)(4,1)}), s8[4194304]{0:T(1024)(128)(4,1)S(1)}, s32[]{:S(2)}) async-start(s8[14155776]{0:T(1024)(128)(4,1)} %bitcast.259), calls=%async_computation.33 | async-start | bytes 8388608
  1193.6 37.1 %slice-start.11 = ((s8[14155776]{0:T(1024)(128)(4,1)}), s8[4194304]{0:T(1024)(128)(4,1)S(1)}, s32[]{:S(2)}) async-start(s8[14155776]{0:T(1024)(128)(4,1)} %bitcast.259), calls=%async_computation.34 | async-start | bytes 8388608
  1232.0 34.7 %copy-start.52 = (f32[2,768,144]{1,2,0:T(8,128)S(1)}, f32[2,768,144]{1,2,0:T(8,128)}, u32[]{:S(2)}) copy-start(f32[2,768,144]{1,2,0:T(8,128)} %param.21) | copy-start | bytes 2654212
  1244.9 26.6 %copy-start.18 = (f32[2,768,144]{1,2,0:T(8,128)S(1)}, f32[2,768,144]{1,2,0:T(8,128)}, u32[]{:S(2)}) copy-start(f32[2,768,144]{1,2,0:T(8,128)} %param.19) | copy-start | bytes 2654212
  (87 other events, 694.7 us)
Sparse Core Ops, SparseCore 0:
  10.5 35.1 all-gather.14
  56.1 241.1 all-gather.16
  351.6 33.8 all-gather.20
  387.9 32.8 all-gather.18
  437.9 53.0 all-reduce.11
  513.9 52.9 all-reduce.9
  580.2 61.1 reduce-scatter.12
  645.1 61.7 reduce-scatter.10
  738.7 32.2 all-gather.22
  772.8 32.3 all-gather.24
  830.0 53.6 all-reduce.7
  919.4 45.6 reduce-scatter.14
  969.1 45.7 reduce-scatter.16
  1089.8 100.7 reduce-scatter.18
  1193.7 32.8 reduce-scatter.22
  1228.9 37.7 reduce-scatter.20
where the time goes:
time: 1300 us; the launch traced here: 1290 us
  waiting for transfers between devices  675 us (52%)
  matrix products  265 us (20%)
  other arithmetic  174 us (13%)
  local copies, waits for them, and re-layouts  120 us (9%)
  blocking collectives  34.1 us (3%)
  between operations  17.2 us (1%)
    all_gather x1, waiting for transfers between devices, per_device(): lax.all_gather(wide_each[0], 'rows', axis=0, tiled=True)  215 us
    reduce_scatter x1, waiting for transfers between devices, per_device(): lax.psum_scatter(slot_grads.astype(jnp.bfloat16), 'keys', scatter_dimensi...  94.3 us
    reduce_scatter x2, waiting for transfers between devices, per_device(): lax.psum_scatter(jnp.einsum('rhji,rjhd->irhd', soft_low, values_own, pref...  90.3 us
    convert_element_type x2, other arithmetic, per_device(): (soft_again * (grad_soft - row_dots[:, :, None, :])).astype(jnp.bfloat16)  60.2 us
    pmax x1, waiting for transfers between devices, per_device(): lax.pmax(local_top.astype(jnp.bfloat16), 'keys').astype(local_top.dtype)  53.2 us
    psum x1, waiting for transfers between devices, per_device(): lax.psum(jnp.sum(jnp.where(allowed, jnp.exp(raw_scores - row_top[:, :, No...  52.9 us
    psum x1, waiting for transfers between devices, per_device(): row_dots = lax.psum(jnp.sum(soft_again * grad_soft, axis=2), 'keys')  51.8 us
    all_gather x2, waiting for transfers between devices, per_device(): lax.all_gather(queries_own, 'keys', axis=1, tiled=True)  47.9 us
  transfers between devices with their start and end apart: 16, of which 14 were waited for; matrix products, arithmetic and copies ran while one was open for 20% of the time, Pallas kernels for 0%

commit v1 on v0

v1 whole, which is shorter than its diff:
```python
import functools
import math

import jax
import jax.numpy as jnp
from jax import lax
from jax.experimental import pallas as pl
from jax.experimental.pallas import tpu as pltpu
from jax.sharding import PartitionSpec as P

MODEL_WIDTH = 768
H = 12
HD = 64
FF = 3072
BLOCK_COLUMNS = 1152
GAIN_ROW_WIDTH = 1152

EPS_NORM = 1e-06
BETA_ONE = 0.95
BETA_TWO = 0.95
EPS_ADAM = 1e-08
DECAY = 0.01
RATE_SMALL = 0.3
NEG_BIG = -1e30
NEG_FLOOR = -1e29
HIGHEST_PREC = lax.Precision.HIGHEST
MESH = pl.DeviceIdType.MESH
F32 = jnp.float32
BF16 = jnp.bfloat16
ANY = pl.BlockSpec(memory_space=pl.ANY)
VMEM_SPEC = pl.BlockSpec(memory_space=pltpu.VMEM)
EXT = 16


def layer_norm(value):
    mean_val = jnp.mean(value, axis=-1, keepdims=True)
    centered = value - mean_val
    inv_dev = lax.rsqrt(jnp.mean(centered * centered, axis=-1, keepdims=True) + EPS_NORM)
    return (centered * inv_dev, inv_dev)


def norm_back(grad_in, normed, inv_dev, gain):
    scaled = grad_in * gain
    return inv_dev * (
        scaled
        - jnp.mean(scaled, axis=-1, keepdims=True)
        - normed * jnp.mean(scaled * normed, axis=-1, keepdims=True)
    )


def inverse_order(owners):
    slot_index_list = jnp.arange(owners.shape[0], dtype=jnp.int32)
    matches = (owners[None, :] == slot_index_list[:, None]).astype(jnp.int32)
    return jnp.sum(matches * slot_index_list[None, :], axis=1)


def column_rates(columns):
    inner = MODEL_WIDTH ** (-0.5)
    return jnp.where(
        columns < 3 * MODEL_WIDTH,
        inner,
        jnp.where(
            columns < 4 * MODEL_WIDTH,
            4.0 * inner,
            jnp.where(columns < 4 * MODEL_WIDTH + FF, inner, FF ** (-0.5)),
        ),
    )


def dot_f32(left, right, contract):
    return lax.dot_general(left, right, (contract, ((), ())), preferred_element_type=F32)


class Place:
    def __init__(self, side_y, side_x, rows):
        self.Y, self.X, self.R = side_y, side_x, rows
        key = lax.axis_index("keys")
        self.key = key
        self.r = lax.axis_index("rows")
        self.c = lax.rem(key, 2)
        self.x = lax.rem(key // 2, side_x)
        self.y = key // (2 * side_x)

    def keyof(self, y, x, c):
        return (y * self.X + x) * 2 + c

    def xo(self, d):
        return lax.rem(self.x + d, self.X)

    def yo(self, d):
        return lax.rem(self.y + d, self.Y)

    def ro(self, d):
        return lax.rem(self.r + d, self.R)

    def x_peer(self, d):
        return {"keys": self.keyof(self.y, self.xo(d), self.c)}

    def y_peer(self, d):
        return {"keys": self.keyof(self.yo(d), self.x, self.c)}

    def core_peer(self):
        return {"keys": self.keyof(self.y, self.x, 1 - self.c)}

    def z_peer(self, d):
        return {"rows": self.ro(d)}

    def barrier(self, with_z):
        sem = pltpu.get_barrier_semaphore()
        peers = [self.core_peer()]
        peers += [self.x_peer(d) for d in range(1, self.X)]
        peers += [self.y_peer(d) for d in range(1, self.Y)]
        if with_z:
            peers += [self.z_peer(d) for d in range(1, self.R)]
        for peer in peers:
            pl.semaphore_signal(sem, inc=1, device_id=peer, device_id_type=MESH)
        pl.semaphore_wait(sem, len(peers))


def remote(src, dst, send_sem, recv_sem, peer):
    return pltpu.make_async_remote_copy(
        src_ref=src,
        dst_ref=dst,
        send_sem=send_sem,
        recv_sem=recv_sem,
        device_id=peer,
        device_id_type=MESH,
    )


def sems_per_item(Y, X):
    return (X - 1) + (Y - 1) + 1


class Gather:
    def __init__(self, place, own, buf, send, recv, base, x_first):
        p = place
        self.sent = []
        n = sems_per_item(p.Y, p.X)
        idx = iter(range(base, base + n))
        first = [(p.x_peer(d)) for d in range(1, p.X)] if x_first else [p.y_peer(d) for d in range(1, p.Y)]
        second = [p.y_peer(d) for d in range(1, p.Y)] if x_first else [p.x_peer(d) for d in range(1, p.X)]
        line = buf.at[p.y, :, p.c] if x_first else buf.at[:, p.x, p.c]
        plane = buf.at[:, :, p.c]
        mine = buf.at[p.y, p.x, p.c]
        self.one = []
        for peer in first:
            i = next(idx)
            self.one.append(remote(own, mine, send.at[i], recv.at[i], peer))
        self.two = []
        for peer in second:
            i = next(idx)
            self.two.append(remote(line, line, send.at[i], recv.at[i], peer))
        i = next(idx)
        self.three = [remote(plane, plane, send.at[i], recv.at[i], p.core_peer())]

    def start1(self):
        for copy in self.one:
            copy.start()

    def start2(self):
        for copy in self.one:
            copy.wait_recv()
        for copy in self.two:
            copy.start()

    def start3(self):
        for copy in self.two:
            copy.wait_recv()
        for copy in self.three:
            copy.start()

    def finish(self):
        for copy in self.three:
            copy.wait_recv()
        for copy in self.one + self.two + self.three:
            copy.wait_send()


def gather_weights_kernel(
    Y, X, R, owners, w_ref, ext_ref, x_ref, wt_out, ext_out, xg_out,
    zbuf, zext, stage, sext, zsend, zrecv, send, recv, loc,
):
    p = Place(Y, X, R)
    slots_here = w_ref.shape[0]
    blocks = zbuf.shape[0]
    micro = x_ref.shape[0]
    n = sems_per_item(Y, X)
    p.barrier(True)
    zcopies = []
    here = pl.ds(p.r * slots_here, slots_here)
    for d in range(1, R):
        a = remote(w_ref, zbuf.at[here], zsend.at[d, 0], zrecv.at[d, 0], p.z_peer(d))
        a.start()
        b = remote(ext_ref, zext.at[p.r], zsend.at[d, 1], zrecv.at[d, 1], p.z_peer(d))
        b.start()
        zcopies += [a, b]
    xitems = []
    xlocal = []
    for m in range(micro):
        item = Gather(p, x_ref.at[m], xg_out.at[m], send, recv, m * n, m % 2 == 0)
        item.start1()
        xitems.append(item)
        copy = pltpu.make_async_copy(x_ref.at[m], xg_out.at[m, p.y, p.x, p.c], loc.at[m])
        copy.start()
        xlocal.append(copy)
    wl = pltpu.make_async_copy(w_ref, zbuf.at[here], loc.at[micro])
    wl.start()
    el = pltpu.make_async_copy(ext_ref, zext.at[p.r], loc.at[micro + 1])
    el.start()
    for m in range(micro):
        xlocal[m].wait()
        xitems[m].start2()
    wl.wait()
    el.wait()
    for copy in zcopies:
        copy.wait_recv()
    sext[...] = jnp.sum(zext[...].astype(F32), axis=0).astype(BF16)

    def reorder(b, carry):
        stage[b] = zbuf[owners[b]]
        return carry

    lax.fori_loop(0, blocks, reorder, 0)
    base = micro * n
    eitem = Gather(p, sext, ext_out, send, recv, base, True)
    base += n
    eitem.start1()
    lcopies = []
    ecopy = pltpu.make_async_copy(sext, ext_out.at[p.y, p.x, p.c], loc.at[micro + 2])
    ecopy.start()
    items = []
    for b in range(blocks):
        item = Gather(p, stage.at[b], wt_out.at[b], send, recv, base, b % 2 == 0)
        base += n
        item.start1()
        items.append(item)
        copy = pltpu.make_async_copy(stage.at[b], wt_out.at[b, p.y, p.x, p.c], loc.at[micro + 3 + b])
        copy.start()
        lcopies.append(copy)
    for m in range(micro):
        xitems[m].start3()
    ecopy.wait()
    eitem.start2()
    for b in range(blocks):
        lcopies[b].wait()
        items[b].start2()
    eitem.start3()
    for b in range(blocks):
        items[b].start3()
    for item in xitems + [eitem] + items:
        item.finish()
    for copy in zcopies:
        copy.wait_send()


def gather_weights(mesh_dims, owners, w_own, ext, x_own):
    Y, X, R = mesh_dims
    slots_here, n, width = w_own.shape
    micro, tok = x_own.shape[:2]
    blocks = slots_here * R
    total = sems_per_item(Y, X) * (micro + 1 + blocks)
    return pl.pallas_call(
        functools.partial(gather_weights_kernel, Y, X, R),
        out_shape=(
            jax.ShapeDtypeStruct((blocks, Y, X, 2, n, width), BF16),
            jax.ShapeDtypeStruct((Y, X, 2, EXT, width), BF16),
            jax.ShapeDtypeStruct((micro, Y, X, 2, tok, width), BF16),
        ),
        in_specs=[pl.BlockSpec(memory_space=pltpu.SMEM), ANY, ANY, ANY],
        out_specs=(ANY, ANY, ANY),
        scratch_shapes=[
            pltpu.VMEM((blocks, n, width), BF16),
            pltpu.VMEM((R, EXT, width), BF16),
            pltpu.VMEM((blocks, n, width), BF16),
            pltpu.VMEM((EXT, width), BF16),
            pltpu.SemaphoreType.DMA((R, 2)),
            pltpu.SemaphoreType.DMA((R, 2)),
            pltpu.SemaphoreType.DMA((total,)),
            pltpu.SemaphoreType.DMA((total,)),
            pltpu.SemaphoreType.DMA((micro + 3 + blocks,)),
        ],
        compiler_params=pltpu.CompilerParams(
            collective_id=1, has_side_effects=True, vmem_limit_bytes=40 << 20
        ),
        name="gather_weights",
    )(owners, w_own, ext, x_own)


class Scatter:
    def __init__(self, place, parts, accs, r1s, r2s, r3s, send, recv, loc, base, lbase, y_first, merge):
        p = place
        self.p, self.y_first, self.merge = p, y_first, merge
        self.accs, self.r1s, self.r2s, self.r3s = accs, r1s, r2s, r3s
        self.count = len(parts)
        n = sems_per_item(p.Y, p.X) * len(parts)
        idx = iter(range(base, base + n))
        self.zero, self.one, self.two, self.three = [], [], [], []
        for t, part in enumerate(parts):
            i = next(idx)
            self.zero.append(pltpu.make_async_copy(part.at[:, :, p.c], accs[t], loc.at[lbase + t]))
            self.one.append(remote(part.at[:, :, 1 - p.c], r1s[t], send.at[i], recv.at[i], p.core_peer()))
            if y_first:
                for d in range(1, p.Y):
                    i = next(idx)
                    self.two.append(
                        remote(accs[t].at[p.yo(d)], r2s[t].at[d - 1], send.at[i], recv.at[i], p.y_peer(d))
                    )
                for d in range(1, p.X):
                    i = next(idx)
                    self.three.append(
                        remote(accs[t].at[p.y, p.xo(d)], r3s[t].at[d - 1], send.at[i], recv.at[i], p.x_peer(d))
                    )
            else:
                for d in range(1, p.X):
                    i = next(idx)
                    self.two.append(
                        remote(accs[t].at[:, p.xo(d)], r2s[t].at[d - 1], send.at[i], recv.at[i], p.x_peer(d))
                    )
                for d in range(1, p.Y):
                    i = next(idx)
                    self.three.append(
                        remote(accs[t].at[p.yo(d), p.x], r3s[t].at[d - 1], send.at[i], recv.at[i], p.y_peer(d))
                    )

    def start1(self):
        for copy in self.zero + self.one:
            copy.start()

    def start2(self):
        p = self.p
        for copy in self.zero:
            copy.wait()
        for copy in self.one:
            copy.wait_recv()

        def body(i, carry):
            y, x = i // p.X, lax.rem(i, p.X)
            self.merge([a.at[y, x] for a in self.accs], [r.at[y, x] for r in self.r1s])
            return carry

        lax.fori_loop(0, p.Y * p.X, body, 0)
        for copy in self.two:
            copy.start()

    def start3(self):
        p = self.p
        for copy in self.two:
            copy.wait_recv()
        if self.y_first:
            for d in range(1, p.Y):
                for x in range(p.X):
                    self.merge([a.at[p.y, x] for a in self.accs], [r.at[d - 1, x] for r in self.r2s])
        else:
            for d in range(1, p.X):
                for y in range(p.Y):
                    self.merge([a.at[y, p.x] for a in self.accs], [r.at[d - 1, y] for r in self.r2s])
        for copy in self.three:
            copy.start()

    def finish(self):
        p = self.p
        for copy in self.three:
            copy.wait_recv()
        mine = [a.at[p.y, p.x] for a in self.accs]
        for d in range(1, p.X if self.y_first else p.Y):
            self.merge(mine, [r.at[d - 1] for r in self.r3s])
        return mine

    def drain(self):
        for copy in self.one + self.two + self.three:
            copy.wait_send()


def merge_sum(into, other):
    a, b = into[0], other[0]
    a[...] = (a[...].astype(F32) + b[...].astype(F32)).astype(BF16)


def merge_soft(into, other):
    (va, sa), (vb, sb) = into, other
    ta, tb = sa[...], sb[...]
    heads = ta.shape[0] // 2
    top_a, top_b = ta[:heads], tb[:heads]
    top = jnp.maximum(top_a, top_b)
    wa, wb = jnp.exp(top_a - top), jnp.exp(top_b - top)
    sa[...] = jnp.concatenate([top, wa * ta[heads:] + wb * tb[heads:]], axis=0)
    for h in range(heads):
        rows = slice(h * HD, (h + 1) * HD)
        va[rows, :] = (
            va[rows, :].astype(F32) * wa[h : h + 1] + vb[rows, :].astype(F32) * wb[h : h + 1]
        ).astype(BF16)


def scatter_scratch(Y, X, items, shape, dtype, y_first_of):
    most = max((Y - 1) * X, (X - 1) * Y)
    return [
        pltpu.VMEM((items, Y, X) + shape, dtype),
        pltpu.VMEM((items, Y, X) + shape, dtype),
        pltpu.VMEM((items, max(Y, X) - 1, max(Y, X)) + shape, dtype),
        pltpu.VMEM((items, max(Y, X) - 1) + shape, dtype),
    ]


GROUP = 4


def merge_attention_kernel(
    Y, X, R, o_ref, st_ref, att_out, st_out,
    oa, o1, o2, o3, sa, s1, s2, s3, send, recv, loc,
):
    p = Place(Y, X, R)
    micro = o_ref.shape[0]
    groups = st_ref.shape[1]
    rows = GROUP * HD
    n = sems_per_item(Y, X) * 2
    p.barrier(False)
    items = []
    for g in range(groups):
        for m in range(micro):
            i = m * groups + g
            item = Scatter(
                p,
                [o_ref.at[m, :, :, :, pl.ds(g * rows, rows)], st_ref.at[m, g]],
                [oa.at[i], sa.at[i]],
                [o1.at[i], s1.at[i]],
                [o2.at[i], s2.at[i]],
                [o3.at[i], s3.at[i]],
                send, recv, loc, i * n, i * 2, m % 2 == 0, merge_soft,
            )
            item.start1()
            items.append((m, g, item))
    for m, g, item in items:
        item.start2()
    for m, g, item in items:
        item.start3()
    for m, g, item in items:
        val, st = item.finish()
        tile = st[...]
        inv = 1.0 / tile[GROUP:]
        st_out[m, g] = jnp.concatenate([tile[:GROUP], inv], axis=0)
        for h in range(GROUP):
            att_out[m, g * rows + h * HD : g * rows + (h + 1) * HD, :] = (
                val[h * HD : (h + 1) * HD, :].astype(F32) * inv[h : h + 1]
            ).astype(BF16)
    for m, g, item in items:
        item.drain()


def merge_attention(mesh_dims, o_part, st_part):
    Y, X, R = mesh_dims
    micro, width, tok = o_part.shape[0], o_part.shape[4], o_part.shape[5]
    groups = st_part.shape[1]
    items = micro * groups
    total = sems_per_item(Y, X) * 2 * items
    return pl.pallas_call(
        functools.partial(merge_attention_kernel, Y, X, R),
        out_shape=(
            jax.ShapeDtypeStruct((micro, width, tok), BF16),
            jax.ShapeDtypeStruct((micro, groups, 2 * GROUP, tok), F32),
        ),
        in_specs=[ANY, ANY],
        out_specs=(VMEM_SPEC, VMEM_SPEC),
        scratch_shapes=scatter_scratch(Y, X, items, (GROUP * HD, tok), BF16, None)
        + scatter_scratch(Y, X, items, (2 * GROUP, tok), F32, None)
        + [
            pltpu.SemaphoreType.DMA((total,)),
            pltpu.SemaphoreType.DMA((total,)),
            pltpu.SemaphoreType.DMA((items * 2,)),
        ],
        compiler_params=pltpu.CompilerParams(
            collective_id=2, has_side_effects=True, vmem_limit_bytes=40 << 20
        ),
        name="merge_attention",
    )(o_part, st_part)


def gather_grads_kernel(Y, X, R, d_ref, st_ref, d_out, st_out, send, recv, loc):
    p = Place(Y, X, R)
    micro, groups = st_ref.shape[:2]
    rows = GROUP * HD
    n = sems_per_item(Y, X)
    p.barrier(False)
    items, local = [], []
    i = 0
    for g in range(groups):
        for m in range(micro):
            ds = pl.ds(g * rows, rows)
            for own, out in (
                (d_ref.at[m, ds], d_out.at[m, :, :, :, ds]),
                (st_ref.at[m, g], st_out.at[m, g]),
            ):
                item = Gather(p, own, out, send, recv, i * n, m % 2 == 0)
                item.start1()
                items.append(item)
                copy = pltpu.make_async_copy(own, out.at[p.y, p.x, p.c], loc.at[i])
                copy.start()
                local.append(copy)
                i += 1
    for item, copy in zip(items, local):
        copy.wait()
        item.start2()
    for item in items:
        item.start3()
    for item in items:
        item.finish()


def gather_grads(mesh_dims, datt, st):
    Y, X, R = mesh_dims
    micro, width, tok = datt.shape
    groups, strows = st.shape[1:3]
    items = micro * groups * 2
    total = sems_per_item(Y, X) * items
    return pl.pallas_call(
        functools.partial(gather_grads_kernel, Y, X, R),
        out_shape=(
            jax.ShapeDtypeStruct((micro, Y, X, 2, width, tok), BF16),
            jax.ShapeDtypeStruct((micro, groups, Y, X, 2, strows, tok), F32),
        ),
        in_specs=[ANY, ANY],
        out_specs=(ANY, ANY),
        scratch_shapes=[
            pltpu.SemaphoreType.DMA((total,)),
            pltpu.SemaphoreType.DMA((total,)),
            pltpu.SemaphoreType.DMA((items,)),
        ],
        compiler_params=pltpu.CompilerParams(collective_id=3, has_side_effects=True),
        name="gather_grads",
    )(datt, st)


def scatter_queries_kernel(Y, X, R, dq_ref, dq_out, a, r1, r2, r3, send, recv, loc):
    p = Place(Y, X, R)
    micro = dq_ref.shape[0]
    groups = a.shape[0] // micro
    rows = GROUP * HD
    n = sems_per_item(Y, X)
    p.barrier(False)
    items = []
    for g in range(groups):
        for m in range(micro):
            i = m * groups + g
            item = Scatter(
                p, [dq_ref.at[m, :, :, :, pl.ds(g * rows, rows)]],
                [a.at[i]], [r1.at[i]], [r2.at[i]], [r3.at[i]],
                send, recv, loc, i * n, i, m % 2 == 0, merge_sum,
            )
            item.start1()
            items.append((m, g, item))
    for m, g, item in items:
        item.start2()
    for m, g, item in items:
        item.start3()
    for m, g, item in items:
        (val,) = item.finish()
        dq_out[m, g * rows : (g + 1) * rows, :] = val[...]
    for m, g, item in items:
        item.drain()


def scatter_queries(mesh_dims, dq_part):
    Y, X, R = mesh_dims
    micro, width, tok = dq_part.shape[0], dq_part.shape[4], dq_part.shape[5]
    groups = width // (GROUP * HD)
    items = micro * groups
    total = sems_per_item(Y, X) * items
    return pl.pallas_call(
        functools.partial(scatter_queries_kernel, Y, X, R),
        out_shape=jax.ShapeDtypeStruct((micro, width, tok), BF16),
        in_specs=[ANY],
        out_specs=VMEM_SPEC,
        scratch_shapes=scatter_scratch(Y, X, items, (GROUP * HD, tok), BF16, None)
        + [
            pltpu.SemaphoreType.DMA((total,)),
            pltpu.SemaphoreType.DMA((total,)),
            pltpu.SemaphoreType.DMA((items,)),
        ],
        compiler_params=pltpu.CompilerParams(
            collective_id=4, has_side_effects=True, vmem_limit_bytes=40 << 20
        ),
        name="scatter_queries",
    )(dq_part)


def scatter_weights_kernel(
    Y, X, R, inverse, g_ref, e_ref, g_out, e_out,
    a, r1, r2, r3, ea, e1, e2, e3, stage, rz, ez, send, recv, loc, zsend, zrecv,
):
    p = Place(Y, X, R)
    blocks = g_ref.shape[0]
    slots_here = g_out.shape[0]
    n = sems_per_item(Y, X)
    p.barrier(True)
    items = []
    for b in range(blocks):
        item = Scatter(
            p, [g_ref.at[b]], [a.at[b]], [r1.at[b]], [r2.at[b]], [r3.at[b]],
            send, recv, loc, b * n, b, b % 2 == 0, merge_sum,
        )
        item.start1()
        items.append(item)
    eitem = Scatter(
        p, [e_ref], [ea.at[0]], [e1.at[0]], [e2.at[0]], [e3.at[0]],
        send, recv, loc, blocks * n, blocks, True, merge_sum,
    )
    eitem.start1()
    for item in items + [eitem]:
        item.start2()
    for item in items + [eitem]:
        item.start3()
    for item in items + [eitem]:
        item.finish()
    fin = a.at[:, p.y, p.x]

    def reorder(s, carry):
        stage[s] = fin[inverse[s]]
        return carry

    lax.fori_loop(0, blocks, reorder, 0)
    emine = ea.at[0, p.y, p.x]
    zcopies = []
    for d in range(1, R):
        there = pl.ds(p.ro(d) * slots_here, slots_here)
        copy = remote(stage.at[there], rz.at[d - 1], zsend.at[d, 0], zrecv.at[d, 0], p.z_peer(d))
        copy.start()
        zcopies.append(copy)
        copy = remote(emine, ez.at[d - 1], zsend.at[d, 1], zrecv.at[d, 1], p.z_peer(d))
        copy.start()
        zcopies.append(copy)
    for item in items + [eitem]:
        item.drain()
    for copy in zcopies:
        copy.wait_recv()
    e_out[...] = emine[...].astype(F32) + jnp.sum(ez[...].astype(F32), axis=0)
    for s in range(slots_here):
        total = stage[p.r * slots_here + s].astype(F32)
        for d in range(1, R):
            total = total + rz[d - 1, s].astype(F32)
        g_out[s] = total
    for copy in zcopies:
        copy.wait_send()


def scatter_weights(mesh_dims, inverse, grads, ext):
    Y, X, R = mesh_dims
    blocks, n, width = grads.shape[0], grads.shape[4], grads.shape[5]
    slots_here = blocks // R
    per = sems_per_item(Y, X)
    return pl.pallas_call(
        functools.partial(scatter_weights_kernel, Y, X, R),
        out_shape=(
            jax.ShapeDtypeStruct((slots_here, n, width), F32),
            jax.ShapeDtypeStruct((EXT, width), F32),
        ),
        in_specs=[pl.BlockSpec(memory_space=pltpu.SMEM), ANY, ANY],
        out_specs=(VMEM_SPEC, VMEM_SPEC),
        scratch_shapes=scatter_scratch(Y, X, blocks, (n, width), BF16, None)
        + scatter_scratch(Y, X, 1, (EXT, width), BF16, None)
        + [
            pltpu.VMEM((blocks, n, width), BF16),
            pltpu.VMEM((R - 1, slots_here, n, width), BF16),
            pltpu.VMEM((R - 1, EXT, width), BF16),
            pltpu.SemaphoreType.DMA((per * (blocks + 1),)),
            pltpu.SemaphoreType.DMA((per * (blocks + 1),)),
            pltpu.SemaphoreType.DMA((blocks + 1,)),
            pltpu.SemaphoreType.DMA((R, 2)),
            pltpu.SemaphoreType.DMA((R, 2)),
        ],
        compiler_params=pltpu.CompilerParams(
            collective_id=5, has_side_effects=True, vmem_limit_bytes=48 << 20
        ),
        name="scatter_weights",
    )(inverse, grads, ext)


def attention_forward_kernel(
    q_ref, k_ref, v_ref, prev_ref, segk_ref, segq_ref,
    logit_ref, e_ref, o_ref, st_ref, top_ref, mask_ref,
):
    h = pl.program_id(1)
    chunks, wide = o_ref.shape[1], o_ref.shape[3]

    @pl.when(h == 0)
    def _():
        mask_ref[...] = jnp.where(segk_ref[0] == segq_ref[0], 0.0, NEG_BIG)

    hg = lax.rem(h, GROUP)
    k_low, v_low = k_ref[...], v_ref[...]
    for t in range(chunks):
        cols = slice(t * wide, (t + 1) * wide)
        score = dot_f32(k_low, q_ref[:, cols], ((0,), (0,)))
        raw = score + prev_ref[0, 0, 0, :, cols].astype(F32)
        logit_ref[0, 0, 0, :, cols] = raw.astype(BF16)
        masked = raw + mask_ref[:, cols]
        top = jnp.maximum(jnp.max(masked, axis=0, keepdims=True), NEG_FLOOR)
        expo = jnp.exp(masked - top)
        total = jnp.sum(expo, axis=0, keepdims=True)
        low = expo.astype(BF16)
        e_ref[0, 0, :, cols] = low
        o_ref[0, t] = dot_f32(v_low, low, ((1,), (0,))).astype(BF16)
        st_ref[0, 0, t, pl.ds(hg, 1), :] = top
        st_ref[0, 0, t, pl.ds(GROUP + hg, 1), :] = total
        top_ref[0, 0, t, pl.ds(hg, 1), :] = top


def attention_forward(q_all, k_all, v_all, prev, segk, segq, chunks, wide):
    micro, _, heads, own, slots = prev.shape
    groups = heads // GROUP
    flops = micro * heads * 2 * 2 * own * slots * HD
    head = lambda m, h: (h, m)
    return pl.pallas_call(
        attention_forward_kernel,
        grid=(micro, heads),
        out_shape=(
            jax.ShapeDtypeStruct(prev.shape, BF16),
            jax.ShapeDtypeStruct((micro, heads, own, slots), BF16),
            jax.ShapeDtypeStruct((micro, chunks, heads * HD, wide), BF16),
            jax.ShapeDtypeStruct((micro, groups, chunks, 2 * GROUP, wide), F32),
            jax.ShapeDtypeStruct((micro, groups, chunks, 2 * GROUP, wide), F32),
        ),
        in_specs=[
            pl.BlockSpec((HD, slots), head),
            pl.BlockSpec((None, HD, own), lambda m, h: (m, h, 0)),
            pl.BlockSpec((None, HD, own), lambda m, h: (m, h, 0)),
            pl.BlockSpec((1, 1, 1, own, slots), lambda m, h: (m, 0, h, 0, 0)),
            pl.BlockSpec((1, own, 1), lambda m, h: (m, 0, 0)),
            pl.BlockSpec((1, 1, slots), lambda m, h: (m, 0, 0)),
        ],
        out_specs=(
            pl.BlockSpec((1, 1, 1, own, slots), lambda m, h: (m, 0, h, 0, 0)),
            pl.BlockSpec((1, 1, own, slots), lambda m, h: (m, h, 0, 0)),
            pl.BlockSpec((1, chunks, HD, wide), lambda m, h: (m, 0, h, 0)),
            pl.BlockSpec((1, 1, chunks, 2 * GROUP, wide), lambda m, h: (m, h // GROUP, 0, 0, 0)),
            pl.BlockSpec((1, 1, chunks, 2 * GROUP, wide), lambda m, h: (m, h // GROUP, 0, 0, 0)),
        ),
        scratch_shapes=[pltpu.VMEM((own, slots), F32)],
        compiler_params=pltpu.CompilerParams(vmem_limit_bytes=32 << 20),
        cost_estimate=pl.CostEstimate(
            flops=flops, bytes_accessed=micro * heads * own * slots * 6, transcendentals=micro * heads * own * slots
        ),
        name="attention_forward",
    )(q_all, k_all, v_all, prev, segk, segq)


def attention_backward_kernel(
    scale, e_ref, d_ref, st_ref, top_ref, q_ref, k_ref, v_ref, g_ref, dq_ref, dk_ref, dv_ref
):
    h = pl.program_id(1)
    chunks, wide = d_ref.shape[1], d_ref.shape[3]
    hg = lax.rem(h, GROUP)
    k_low, v_low = k_ref[...], v_ref[...]
    dk = jnp.zeros(dk_ref.shape[1:], F32)
    dv = jnp.zeros(dv_ref.shape[1:], F32)
    for t in range(chunks):
        cols = slice(t * wide, (t + 1) * wide)
        top = st_ref[0, 0, t, pl.ds(hg, 1), :]
        inv = st_ref[0, 0, t, pl.ds(GROUP + hg, 1), :]
        dots = st_ref[0, 0, t, pl.ds(2 * GROUP + hg, 1), :]
        weight = jnp.exp(top_ref[0, 0, t, pl.ds(hg, 1), :] - top) * inv
        low = e_ref[0, 0, :, cols]
        grad_in = (d_ref[0, t].astype(F32) * weight).astype(BF16)
        soft = dot_f32(v_low, grad_in, ((0,), (0,))) - dots * weight
        grad = (low.astype(F32) * soft).astype(BF16)
        g_ref[0, 0, 0, :, cols] = grad
        dq_ref[0, t] = (dot_f32(k_low, grad, ((1,), (0,))) * scale).astype(BF16)
        dv = dv + dot_f32(grad_in, low, ((1,), (1,)))
        dk = dk + dot_f32(q_ref[:, cols], grad, ((1,), (1,)))
    dk_ref[0] = dk.astype(BF16)
    dv_ref[0] = dv.astype(BF16)


def attention_backward(expo, datt, st, tops, q_all, k_all, v_all, scale):
    micro, heads, own, slots = expo.shape
    chunks, wide = datt.shape[1], datt.shape[3]
    flops = micro * heads * 2 * 4 * own * slots * HD
    sts = st.shape[3]
    return pl.pallas_call(
        functools.partial(attention_backward_kernel, scale),
        grid=(micro, heads),
        out_shape=(
            jax.ShapeDtypeStruct((micro, 1, heads, own, slots), BF16),
            jax.ShapeDtypeStruct((micro, chunks, heads * HD, wide), BF16),
            jax.ShapeDtypeStruct((micro, heads * HD, own), BF16),
            jax.ShapeDtypeStruct((micro, heads * HD, own), BF16),
        ),
        in_specs=[
            pl.BlockSpec((1, 1, own, slots), lambda m, h: (m, h, 0, 0)),
            pl.BlockSpec((1, chunks, HD, wide), lambda m, h: (m, 0, h, 0)),
            pl.BlockSpec((1, 1, chunks, sts, wide), lambda m, h: (m, h // GROUP, 0, 0, 0)),
            pl.BlockSpec((1, 1, chunks, 2 * GROUP, wide), lambda m, h: (m, h // GROUP, 0, 0, 0)),
            pl.BlockSpec((HD, slots), lambda m, h: (h, m)),
            pl.BlockSpec((None, HD, own), lambda m, h: (m, h, 0)),
            pl.BlockSpec((None, HD, own), lambda m, h: (m, h, 0)),
        ],
        out_specs=(
            pl.BlockSpec((1, 1, 1, own, slots), lambda m, h: (m, 0, h, 0, 0)),
            pl.BlockSpec((1, chunks, HD, wide), lambda m, h: (m, 0, h, 0)),
            pl.BlockSpec((1, HD, own), lambda m, h: (m, h, 0)),
            pl.BlockSpec((1, HD, own), lambda m, h: (m, h, 0)),
        ),
        compiler_params=pltpu.CompilerParams(vmem_limit_bytes=32 << 20),
        cost_estimate=pl.CostEstimate(
            flops=flops, bytes_accessed=micro * heads * own * slots * 4, transcendentals=0
        ),
        name="attention_backward",
    )(expo, datt, st, tops, q_all, k_all, v_all)


def to_chunks(arr, chunks):
    pieces, rows, own = arr.shape[-3:]
    lead = arr.shape[:-3]
    if pieces == chunks:
        return arr
    per = pieces // chunks
    arr = arr.reshape(lead + (chunks, per, rows, own))
    return jnp.moveaxis(arr, -3, -2).reshape(lead + (chunks, rows, per * own))


def from_chunks(arr, pieces):
    chunks, rows, wide = arr.shape[-3:]
    lead = arr.shape[:-3]
    if pieces == chunks:
        return arr
    per = pieces // chunks
    arr = arr.reshape(lead + (chunks, rows, per, wide // per))
    return jnp.moveaxis(arr, -2, -3).reshape(lead + (pieces, rows, wide // per))


def per_device(
    mesh_dims,
    tokens,
    prev_logits,
    segments,
    out_cot,
    master_mat,
    mom1_mat,
    mom2_mat,
    eigen_bases,
    master_small,
    mom1_small,
    mom2_small,
    owners,
    step_count,
):
    Y, X, R = mesh_dims
    keys = Y * X * 2
    micro, row_count, key_len, width = tokens.shape
    slot_count = prev_logits.shape[4]
    slots_here, _, cols_here = master_mat.shape
    blocks = slots_here * R
    token_count = micro * key_len
    scale = HD ** (-0.5)
    key_index = lax.axis_index("keys")
    row_index = lax.axis_index("rows")
    wide = max(key_len, min(256, slot_count))
    chunks = slot_count // wide
    groups = H // GROUP

    x_own = tokens.reshape(micro, key_len, width)
    w_own = jnp.swapaxes(master_mat, 1, 2).astype(BF16)
    small_low = master_small.astype(BF16).reshape(1, slots_here * cols_here)
    ext = lax.dynamic_update_slice(
        jnp.zeros((EXT, width), BF16), small_low, (row_index, jnp.int32(0))
    )
    wt, ext_all, xg = gather_weights(mesh_dims, owners, w_own, ext, x_own)
    w_t = wt.reshape(blocks * BLOCK_COLUMNS, width)
    small_all = ext_all.reshape(keys, EXT, width)[:, :R, : slots_here * cols_here]
    params = (
        jnp.transpose(small_all.reshape(keys, R, slots_here, cols_here), (1, 2, 0, 3))
        .reshape(blocks * GAIN_ROW_WIDTH)
        .astype(F32)
    )
    wq_t = w_t[:width]
    wkv_t = w_t[width : 3 * width]
    wqkv_t = w_t[: 3 * width]
    wo_t = w_t[3 * width : 4 * width]
    wu_t = w_t[4 * width : 4 * width + FF]
    wd_t = w_t[4 * width + FF :]
    bias_q = params[:width]
    bias_v = params[width : 2 * width]
    bias_o = params[2 * width : 3 * width]
    gain_one = params[3 * width : 4 * width]
    shift_one = params[4 * width : 5 * width]
    bias_up = params[5 * width : 5 * width + FF]
    bias_down = params[5 * width + FF : 6 * width + FF]
    gain_two = params[6 * width + FF : 7 * width + FF]
    shift_two = params[7 * width + FF :]

    q_all = (
        (dot_f32(wq_t, xg.reshape(micro * slot_count, width), ((1,), (1,))) + bias_q[:, None])
        .astype(BF16) * jnp.asarray(scale, BF16)
    )
    x_rows = x_own.reshape(token_count, width)
    kv = dot_f32(wkv_t, x_rows, ((1,), (1,))) + jnp.concatenate([jnp.zeros_like(bias_v), bias_v])[:, None]
    kv = jnp.swapaxes(kv.astype(BF16).reshape(2 * width, micro, key_len), 0, 1)
    k_all, v_all = kv[:, :width], kv[:, width:]

    seg_rows = segments.reshape(micro, slot_count)
    seg_keys = lax.dynamic_slice_in_dim(seg_rows, key_index * key_len, key_len, 1)
    logits, expo, o_part, st_part, tops = attention_forward(
        q_all, k_all, v_all, prev_logits, seg_keys[:, :, None], seg_rows[:, None, :], chunks, wide
    )
    o_part = from_chunks(o_part, keys).reshape(micro, Y, X, 2, width, key_len)
    st_part = from_chunks(st_part, keys).reshape(micro, groups, Y, X, 2, 2 * GROUP, key_len)
    att, st = merge_attention(mesh_dims, o_part, st_part)

    att_t = jnp.swapaxes(att, 0, 1).reshape(width, token_count)
    branch = dot_f32(att_t, wo_t, ((0,), (1,))) + bias_o
    normed_one, inv_one = layer_norm(x_rows.astype(F32) + branch)
    mid_act = normed_one * gain_one + shift_one
    mid_low = mid_act.astype(BF16)
    pre_act = dot_f32(mid_low, wu_t, ((1,), (1,))) + bias_up
    hidden = jax.nn.gelu(pre_act, approximate=False).astype(BF16)
    ffn_out = dot_f32(hidden, wd_t, ((1,), (0,))) + bias_down
    normed_two, inv_two = layer_norm(mid_act + ffn_out)
    out_hidden = (normed_two * gain_two + shift_two).astype(BF16).reshape(tokens.shape)
    grad_out = out_cot.reshape(token_count, width).astype(F32)
    grad_sum_two = norm_back(grad_out, normed_two, inv_two, gain_two)
    d_gain_two = jnp.sum(grad_out * normed_two, axis=0)
    d_shift_two = jnp.sum(grad_out, axis=0)
    grad_ffn = grad_sum_two.astype(BF16)
    d_bias_down = jnp.sum(grad_ffn.astype(F32), axis=0)
    d_down = dot_f32(hidden, grad_ffn, ((0,), (0,)))
    grad_hidden = dot_f32(grad_ffn, wd_t, ((1,), (1,)))
    _, gelu_back = jax.vjp(lambda value: jax.nn.gelu(value, approximate=False), pre_act)
    grad_pre = gelu_back(grad_hidden)[0].astype(BF16)
    d_bias_up = jnp.sum(grad_pre.astype(F32), axis=0)
    d_up = dot_f32(grad_pre, mid_low, ((0,), (0,)))
    grad_mid = grad_sum_two + dot_f32(grad_pre, wu_t, ((1,), (0,)))
    grad_one = norm_back(grad_mid, normed_one, inv_one, gain_one)
    d_gain_one = jnp.sum(grad_mid * normed_one, axis=0)
    d_shift_one = jnp.sum(grad_mid, axis=0)
    grad_branch = grad_one.astype(BF16)
    d_bias_o = jnp.sum(grad_branch.astype(F32), axis=0)
    d_out = dot_f32(grad_branch, att_t, ((0,), (1,)))
    datt = dot_f32(wo_t, grad_branch, ((0,), (1,))).astype(BF16)
    datt = jnp.swapaxes(datt.reshape(width, micro, key_len), 0, 1)
    dots = jnp.sum(
        (datt.astype(F32) * att.astype(F32)).reshape(micro, groups, GROUP, HD, key_len), axis=3
    )
    st_own = jnp.concatenate([st, dots, jnp.zeros_like(dots)], axis=2)
    datt_all, st_all = gather_grads(mesh_dims, datt, st_own)
    datt_all = to_chunks(datt_all.reshape(micro, keys, width, key_len), chunks)
    st_all = to_chunks(st_all.reshape(micro, groups, keys, 4 * GROUP, key_len), chunks)
    grad_prev, dq_part, dk, dv = attention_backward(
        expo, datt_all, st_all, tops, q_all, k_all, v_all, scale
    )
    dq_part = from_chunks(dq_part, keys).reshape(micro, Y, X, 2, width, key_len)
    dq = scatter_queries(mesh_dims, dq_part)

    grad_proj = jnp.swapaxes(jnp.concatenate([dq, dk, dv], axis=1), 0, 1).reshape(
        3 * width, token_count
    )
    d_qkv = dot_f32(grad_proj, x_rows, ((1,), (0,)))
    d_bias_q = jnp.sum(grad_proj[:width].astype(F32), axis=1)
    d_bias_v = jnp.sum(grad_proj[2 * width :].astype(F32), axis=1)
    grad_x = grad_one + dot_f32(grad_proj, wqkv_t, ((0,), (0,)))
    grad_tokens = grad_x.astype(BF16).reshape(tokens.shape)

    grads = jnp.concatenate(
        [d_qkv.astype(BF16), d_out.astype(BF16), d_up.astype(BF16), d_down.astype(BF16)], axis=0
    ).reshape(blocks, Y, X, 2, cols_here, width)
    small = jnp.concatenate(
        [d_bias_q, d_bias_v, d_bias_o, d_gain_one, d_shift_one, d_bias_up, d_bias_down, d_gain_two, d_shift_two]
    ).astype(BF16)
    small = jnp.transpose(
        small.reshape(R, slots_here, keys, cols_here), (2, 0, 1, 3)
    ).reshape(keys, R, slots_here * cols_here)
    small = jnp.pad(small, ((0, 0), (0, EXT - R), (0, width - slots_here * cols_here)))
    inverse = inverse_order(owners)
    mine_t, small_sum = scatter_weights(
        mesh_dims, inverse, grads, small.reshape(Y, X, 2, EXT, width)
    )
    mine_mat = jnp.swapaxes(mine_t, 1, 2)
    mine_small = lax.dynamic_slice_in_dim(small_sum, row_index, 1, 0)[
        :, : slots_here * cols_here
    ].reshape(master_small.shape)

    steps_done = step_count[0].astype(F32)
    fix_one = 1.0 - jnp.power(jnp.asarray(BETA_ONE, F32), steps_done)
    fix_two = 1.0 - jnp.power(jnp.asarray(BETA_TWO, F32), steps_done)
    rotated = jnp.einsum("sed,sec->sdc", eigen_bases, mine_mat, precision=HIGHEST_PREC)
    new_one = BETA_ONE * mom1_mat + (1.0 - BETA_ONE) * rotated
    new_two = BETA_TWO * mom2_mat + (1.0 - BETA_TWO) * rotated * rotated
    direction = new_one / fix_one / (jnp.sqrt(new_two / fix_two) + EPS_ADAM)
    back_rot = jnp.einsum("sdk,skc->sdc", eigen_bases, direction, precision=HIGHEST_PREC)
    slot_index_list = row_index * slots_here + jnp.arange(slots_here, dtype=jnp.int32)
    block_ids = jnp.take(inverse, slot_index_list)
    columns = (
        block_ids[:, None] * (cols_here * keys)
        + key_index * cols_here
        + jnp.arange(cols_here, dtype=jnp.int32)[None, :]
    )
    rates = column_rates(columns)[:, None, :]
    new_master = master_mat - rates * (back_rot + DECAY * master_mat)
    small_one = BETA_ONE * mom1_small + (1.0 - BETA_ONE) * mine_small
    small_two = BETA_TWO * mom2_small + (1.0 - BETA_TWO) * mine_small * mine_small
    new_small = master_small - RATE_SMALL * (small_one / fix_one) / (
        jnp.sqrt(small_two / fix_two) + EPS_ADAM
    )
    return (
        out_hidden,
        logits,
        grad_tokens,
        grad_prev,
        mine_mat,
        new_one,
        new_two,
        new_master,
        new_master.astype(BF16),
        mine_small,
        small_one,
        small_two,
        new_small,
        new_small.astype(BF16),
    )


def solution(mesh):
    chips = mesh.shape["keys"] // 2
    side = math.isqrt(chips)
    dims = (side, side, mesh.shape["rows"]) if side * side == chips else (1, chips, mesh.shape["rows"])
    acts = P(None, "rows", "keys", None)
    scores = P(None, "rows", None, "keys", None)
    mats = P("rows", None, "keys")
    smalls = P("rows", "keys")
    return jax.shard_map(
        functools.partial(per_device, dims),
        mesh=mesh,
        in_specs=(
            acts, scores, P(None, "rows", None), acts, mats, mats, mats,
            P("rows", None, None), smalls, smalls, smalls, P(), P(),
        ),
        out_specs=(acts, scores, acts, scores) + (mats,) * 5 + (smalls,) * 5,
        check_vma=False,
    )
```

time: 1300 us -> 607 us (0.47)
  waiting for transfers between devices: 675 us -> 0 us
  Pallas kernels: 0 us -> 428 us
  matrix products: 265 us -> 87.3 us
  other arithmetic: 174 us -> 50.2 us
  local copies, waits for them, and re-layouts: 120 us -> 30.6 us
  blocking collectives: 34.1 us -> 0 us
  between operations: 17.2 us -> 2.05 us
    pallas_call x0 -> x7, Pallas kernels: none -> 428 us  [the longest x1 108 us: gather_weights(): pl.pallas_call(functools.partial(gather_weights_kernel, Y, X, R), out_sha...]
    all_gather x6 -> x0, waiting for transfers between devices: 309 us -> none  [the longest x1 215 us: per_device(): lax.all_gather(wide_each[0], 'rows', axis=0, tiled=True)]
    reduce_scatter x6 -> x0, waiting for transfers between devices: 208 us -> none  [the longest x1 94.3 us: per_device(): lax.psum_scatter(slot_grads.astype(jnp.bfloat16), 'keys', scatter_dimensi...]
    dot_general x36 -> x13, matrix products: 252 us -> 73.5 us  [dot_f32(): lax.dot_general(left, right, (contract, ((), ())), preferred_element_type...]
    psum x2 -> x0, waiting for transfers between devices: 105 us -> none  [the longest x1 52.9 us: per_device(): lax.psum(jnp.sum(jnp.where(allowed, jnp.exp(raw_scores - row_top[:, :, No...]
    convert_element_type x7 -> x4, other arithmetic: 76.9 us -> 3.29 us  [the longest x1 1.38 us: per_device(): new_small.astype(BF16)]
    pmax x1 -> x0, waiting for transfers between devices: 53.2 us -> none  [per_device(): lax.pmax(local_top.astype(jnp.bfloat16), 'keys').astype(local_top.dtype)]
    another operation x4 -> x0, other arithmetic: 38.8 us -> none  [the longest x1 25.2 us: per_device(): jnp.stack(prev_grads)]
  transfers between devices with their start and end apart: 16 -> 0, of which waited for: 14 -> 0; matrix products, arithmetic and copies ran while one was open for 20% -> 0% of each run, Pallas kernels for 0% -> 0%
where the time goes in v1:
time: 607 us; the launch traced here: 599 us
  Pallas kernels  428 us (71%)
  matrix products  87.3 us (14%)
  other arithmetic  50.2 us (8%)
  local copies, waits for them, and re-layouts  30.6 us (5%)
    pallas_call x1, Pallas kernels, gather_weights(): pl.pallas_call(functools.partial(gather_weights_kernel, Y, X, R), out_sha...  108 us
    pallas_call x1, Pallas kernels, scatter_weights(): pl.pallas_call(functools.partial(scatter_weights_kernel, Y, X, R), out_sh...  108 us
    dot_general x13, matrix products, dot_f32(): lax.dot_general(left, right, (contract, ((), ())), preferred_element_type...  73.5 us
    pallas_call x1, Pallas kernels, attention_forward(): pl.pallas_call(attention_forward_kernel, grid=(micro, heads), out_shape=(...  61.7 us
    pallas_call x1, Pallas kernels, attention_backward(): pl.pallas_call(functools.partial(attention_backward_kernel, scale), grid=...  44.8 us
    pallas_call x1, Pallas kernels, gather_grads(): pl.pallas_call(functools.partial(gather_grads_kernel, Y, X, R), out_shape...  39.4 us
    pallas_call x1, Pallas kernels, merge_attention(): pl.pallas_call(functools.partial(merge_attention_kernel, Y, X, R), out_sh...  34.1 us
    concatenate x1, other arithmetic, per_device(): jnp.concatenate([d_qkv.astype(BF16), d_out.astype(BF16), d_up.astype(BF16...  33.5 us

profile of v1, /device:TPU:8, one launch (start us, length us, event | category | flops | bytes accessed | tf_op | source)
XLA Modules:
  0.0 598.6 jit_solution(69595813435942018)
XLA Ops:
  4.2 1.9 reduce.10
  10.7 108.4 %gather_weights.1 = (bf16[8,2,2,2,144,768]{5,4,3,2,1,0:T(8,128)(2,1)}, bf16[2,2,2,16,768]{4,3,2,1,0:T(8,128)(2,1)S(1)}, bf16[2,2,2,2,256,768]{5,4,3,2,1,0:T(8,128)(2,1)S(1)}) custom-call(s32[8]{0:T(128)S(1)} %copy-done.7, bf16[2,144,768]{2,1,0:T(8,128)(2,1)S(1)} %convert_bitcast_fusion.w_ref, bf16[16,768]{1,0:T(8,128)(2,1)S(1)} %dynamic_update_slice.3.ext_ref, ...), custom_call_target="tpu_custom_call" | custom-call | tf_op jit(solution)/shard_map/gather_weights/pallas_call | solution.py:263
  119.2 2.7 copy-done.8
  123.3 9.4 %fusion.6.q_ref = bf16[768,4096]{1,0:T(8,128)(2,1)} fusion(f32[768]{0:T(1024)S(1)} %get-tuple-element.136, bf16[4096,768]{1,0:T(8,128)(2,1)} %bitcast.99, bf16[9216,768]{1,0:T(8,128)(2,1)} %bitcast.110), kind=kOutput, calls=%fused_computation.20 | convolution fusion | flops 4841275392 | bytes 13765632 | tf_op jit(solution)/shard_map/dot_general | solution.py:71
  133.5 3.1 fusion.15
  138.2 1.6 fusion.59
  139.8 4.7 slice.85
  144.6 61.7 %attention_forward.1 = (bf16[2,1,12,256,2048]{4,3,2,1,0:T(8,128)(2,1)}, bf16[2,12,256,2048]{3,2,1,0:T(8,128)(2,1)}, bf16[2,8,768,256]{3,2,1,0:T(8,128)(2,1)S(1)}...) custom-call(bf16[768,4096]{1,0:T(8,128)(2,1)S(1)} %copy-done, ...), custom_call_target="tpu_custom_call" | custom-call | flops 3221225472 | bytes 75497472 | tf_op jit(solution)/shard_map/attention_forward/pallas_call | solution.py:712
  206.3 34.1 %merge_attention.1 = (bf16[2,768,256]{2,1,0:T(8,128)(2,1)S(1)}, f32[2,3,8,256]{3,2,1,0:T(8,128)S(1)}) custom-call(bf16[2,2,2,2,768,256]{5,4,3,2,1,0:T(8,128)(2,1)S(1)} %bitcast.88, f32[2,3,2,2,2,8,256]{6,5,4,3,2,1,0:T(8,128)S(1)} %bitcast.97), custom_call_target="tpu_custom_call" | custom-call | tf_op jit(solution)/shard_map/merge_attention/pallas_call | solution.py:456
  242.2 2.5 fusion.61
  245.1 20.4 %multiply_convert_fusion = (bf16[512,3072]{1,0:T(8,128)(2,1)S(1)}, f32[512,3072]{1,0:T(8,128)}, f32[512,3072]{1,0:T(8,128)}) fusion(f32[3072]{0:T(1024)S(1)} %copy-done.20, bf16[9216,768]{1,0:T(8,128)(2,1)} %bitcast.113, f32[512,768]{1,0:T(8,128)S(1)} %get-tuple-element.138, f32[768]{0:T(1024)S(1)} %copy-done.28, f32[768]{0:T(1024)S(1)} %get-tuple-element.133, ...), kind=kOutput, calls=%fused_computation.6 | convolution fusion | flops 2521694208 | bytes 22042624 | tf_op jit(solution)/shard_map/dot_general | solution.py:71
  265.5 2.8 fusion.62
  268.7 2.2 fusion.25
  271.4 9.6 %fusion.63 = (bf16[3072]{0:T(1024)(128)(2,1)}, bf16[512,3072]{1,0:T(8,128)(2,1)}) fusion(f32[512,3072]{1,0:T(8,128)} %get-tuple-element.123, bf16[9216,768]{1,0:T(8,128)(2,1)S(1)} %bitcast.117, f32[512,768]{1,0:T(8,128)S(1)} %get-tuple-element.119, f32[512,3072]{1,0:T(8,128)} %get-tuple-element.139, f32[3072]{0:T(1024)S(1)} %copy-done.20), kind=kOutput, calls=%fused_computation.124 | convolution fusion | flops 2441475072 | bytes 22038528 | tf_op jit(solution)/shard_map/dot_general | solution.py:71
  281.0 4.3 convolution_convert_fusion
  285.3 3.5 multiply_reduce_fusion
  289.3 4.7 convolution_convert_fusion.1
  294.0 1.7 convolution_convert_fusion.4
  295.7 2.3 copy.52
  298.0 3.4 convolution_convert_fusion.3
  301.4 2.5 convert_multiply_fusion.1
  307.0 39.4 %gather_grads.1 = (bf16[2,2,2,2,768,256]{5,4,3,2,1,0:T(8,128)(2,1)}, f32[2,3,2,2,2,16,256]{6,5,4,3,2,1,0:T(8,128)}) custom-call(bf16[2,768,256]{2,1,0:T(8,128)(2,1)} %bitcast.101, f32[2,3,16,256]{3,2,1,0:T(8,128)} %maximum_maximum_fusion.st_ref), custom_call_target="tpu_custom_call" | custom-call | tf_op jit(solution)/shard_map/gather_grads/pallas_call | solution.py:515
  346.4 2.8 copy-done.1
  350.3 44.8 %attention_backward.1 = (bf16[2,1,12,256,2048]{4,3,2,1,0:T(8,128)(2,1)}, bf16[2,8,768,256]{3,2,1,0:T(8,128)(2,1)S(1)}, bf16[2,768,256]{2,1,0:T(8,128)(2,1)S(1)}, bf16[2,768,256]{2,1,0:T(8,128)(2,1)S(1)}) custom-call(bf16[2,12,256,2048]{3,2,1,0:T(8,128)(2,1)} %get-tuple-element.39.e_ref, bf16[2,8,768,256]{3,2,1,0:T(8,128)(2,1)S(1)} %bitcast.86, ...), custom_call_target="tpu_custom_call" | custom-call | flops 6442450944 | bytes 50331648 | tf_op jit(solution)/shard_map/attention_backward/pallas_call | solution.py:778
  395.1 31.5 %scatter_queries.1 = bf16[2,768,256]{2,1,0:T(8,128)(2,1)S(1)} custom-call(bf16[2,2,2,2,768,256]{5,4,3,2,1,0:T(8,128)(2,1)S(1)} %bitcast.87), custom_call_target="tpu_custom_call" | custom-call | tf_op jit(solution)/shard_map/scatter_queries/pallas_call | solution.py:568
  427.1 2.5 copy.53
  429.7 6.2 %add_convert_fusion.2 = bf16[512,768]{1,0:T(8,128)(2,1)} fusion(f32[512,768]{1,0:T(8,128)} %copy-done.11, bf16[2304,512]{0,1:T(8,128)(2,1)} %bitcast.107, bf16[2304,768]{1,0:T(8,128)(2,1)} %bitcast.104), kind=kOutput, calls=%fused_computation.47 | convolution fusion | flops 1812725760 | bytes 8257536 | tf_op jit(solution)/shard_map/dot_general | solution.py:71
  438.1 2.1 convolution_convert_fusion.2
  440.1 33.5 %pad_maximum_fusion = bf16[9216,768]{1,0:T(8,128)(2,1)} fusion(bf16[3072,768]{1,0:T(8,128)(2,1)} %convolution_convert_fusion, bf16[3072,768]{1,0:T(8,128)(2,1)} %convolution_convert_fusion.1, bf16[768,768]{1,0:T(8,128)(2,1)S(1)} %copy-done.12, bf16[2304,768]{1,0:T(8,128)(2,1)S(1)} %convolution_convert_fusion.2), kind=kLoop, calls=%fused_computation.1 | loop fusion | flops 56623104 | bytes 28311552 | tf_op jit(solution)/shard_map/concatenate | solution.py:961
  473.6 108.4 %scatter_weights.1 = (f32[2,144,768]{2,1,0:T(8,128)S(1)}, f32[16,768]{1,0:T(8,128)S(1)}) custom-call(s32[8]{0:T(128)S(1)} %select_reduce_fusion.inverse, bf16[8,2,2,2,144,768]{5,4,3,2,1,0:T(8,128)(2,1)} %bitcast.100, bf16[2,2,2,16,768]{4,3,2,1,0:T(8,128)(2,1)S(1)} %bitcast.91), custom_call_target="tpu_custom_call" | custom-call | tf_op jit(solution)/shard_map/scatter_weights/pallas_call | solution.py:650
  583.6 5.4 fusion.38
  589.0 8.4 %fusion.64 = (bf16[2,768,144]{1,2,0:T(8,128)(2,1)}, f32[2,768,144]{1,2,0:T(8,128)}) fusion(f32[2,768,144]{1,2,0:T(8,128)S(1)} %copy-done.15, f32[2,768,768]{2,1,0:T(8,128)} %param.20, f32[2,768,144]{1,2,0:T(8,128)S(1)} %get-tuple-element.168, f32[2,768,144]{1,2,0:T(8,128)S(1)} %get-tuple-element.169, f32[]{:T(128)} %bitcast.33, f32[2,144]{1,0:T(2,128)S(1)} %copy-done.21), kind=kOutput, calls=%fused_computation.125 | convolution fusion | flops 2040422400 | bytes 8701060 | tf_op jit(solution)/shard_map/sdk,skc->sdc/dot_general | solution.py:987
  (135 shorter events, 24.1 us)
Async XLA Ops:
  119.2 2.7 copy-start.8
  123.3 9.4 %copy-start.9 = (bf16[2,1,256,768]{3,2,1,0:T(8,128)(2,1)S(1)}, bf16[2,1,256,768]{3,2,1,0:T(8,128)(2,1)}, u32[]{:S(2)}) copy-start(bf16[2,1,256,768]{3,2,1,0:T(8,128)(2,1)} %param.16) | copy-start | bytes 2359300
  123.3 10.2 %copy-start.3 = (bf16[2,1,256,768]{3,2,1,0:T(8,128)(2,1)S(1)}, bf16[2,1,256,768]{3,2,1,0:T(8,128)(2,1)}, u32[]{:S(2)}) copy-start(bf16[2,1,256,768]{3,2,1,0:T(8,128)(2,1)} %param.13) | copy-start | bytes 2359300
  138.2 6.4 %copy-start = (bf16[768,4096]{1,0:T(8,128)(2,1)S(1)}, bf16[768,4096]{1,0:T(8,128)(2,1)}, u32[]{:S(2)}) copy-start(bf16[768,4096]{1,0:T(8,128)(2,1)} %fusion.6.q_ref) | copy-start | bytes 18874372
  138.2 6.4 %copy-start.6 = (s32[2,1,2048]{2,1,0:T(1,128)S(1)}, s32[2,1,2048]{2,1,0:T(1,128)}, u32[]{:S(2)}) copy-start(s32[2,1,2048]{2,1,0:T(1,128)} %segq_ref.1) | copy-start | bytes 49156
  242.2 2.9 copy-start.20
  242.2 2.9 copy-start.28
  242.2 23.3 %slice-start = ((s8[14155776]{0:T(1024)(128)(4,1)}), s8[4194304]{0:T(1024)(128)(4,1)S(1)}, s32[]{:S(2)}) async-start(s8[14155776]{0:T(1024)(128)(4,1)} %bitcast.114), calls=%async_computation | async-start | bytes 8388608
  245.1 20.4 %slice-start.1 = ((s8[14155776]{0:T(1024)(128)(4,1)}), s8[4194304]{0:T(1024)(128)(4,1)S(1)}, s32[]{:S(2)}) async-start(s8[14155776]{0:T(1024)(128)(4,1)} %bitcast.114), calls=%async_computation.1 | async-start | bytes 8388608
  245.1 20.4 %slice-start.2 = ((s8[14155776]{0:T(1024)(128)(4,1)}), s8[4194304]{0:T(1024)(128)(4,1)S(1)}, s32[]{:S(2)}) async-start(s8[14155776]{0:T(1024)(128)(4,1)} %bitcast.114), calls=%async_computation.2 | async-start | bytes 8388608
  245.1 20.4 %slice-start.3 = ((s8[14155776]{0:T(1024)(128)(4,1)}), s8[1572864]{0:T(1024)(128)(4,1)S(1)}, s32[]{:S(2)}) async-start(s8[14155776]{0:T(1024)(128)(4,1)} %bitcast.114), calls=%async_computation.3 | async-start | bytes 3145728
  245.1 20.4 %copy-start.29 = (f32[768]{0:T(1024)S(1)}, f32[768]{0:T(1024)}, u32[]{:S(2)}) copy-start(f32[768]{0:T(1024)} %get-tuple-element.131) | copy-start | bytes 9220
  265.5 3.1 copy-start.10
  281.0 4.3 copy-start.33
  289.3 4.7 copy-start.11
  295.7 9.7 %copy-start.32 = (f32[16]{0:T(128)S(1)}, f32[16]{0:T(128)}, u32[]{:S(2)}) copy-start(f32[16]{0:T(128)} %pad.15.clone) | copy-start | bytes 196
  346.4 2.8 copy-start.1
  429.6 6.2 %copy-start.19 = (bf16[9216]{0:T(1024)(128)(2,1)S(1)}, bf16[9216]{0:T(1024)(128)(2,1)}, u32[]{:S(2)}) copy-start(bf16[9216]{0:T(1024)(128)(2,1)} %custom-call) | copy-start | bytes 55300
  429.6 6.8 %copy-start.31 = (bf16[768]{0:T(1024)(128)(2,1)S(1)}, bf16[768]{0:T(1024)(128)(2,1)}, u32[]{:S(2)}) copy-start(bf16[768]{0:T(1024)(128)(2,1)} %get-tuple-element.106) | copy-start | bytes 4612
  429.6 7.0 %copy-start.30 = (bf16[768]{0:T(1024)(128)(2,1)S(1)}, bf16[768]{0:T(1024)(128)(2,1)}, u32[]{:S(2)}) copy-start(bf16[768]{0:T(1024)(128)(2,1)} %get-tuple-element.113) | copy-start | bytes 4612
  429.6 7.2 %copy-start.27 = (bf16[3072]{0:T(1024)(128)(2,1)S(1)}, bf16[3072]{0:T(1024)(128)(2,1)}, u32[]{:S(2)}) copy-start(bf16[3072]{0:T(1024)(128)(2,1)} %get-tuple-element.143) | copy-start | bytes 18436
  429.6 7.7 %copy-start.24 = (bf16[768]{0:T(1024)(128)(2,1)S(1)}, bf16[768]{0:T(1024)(128)(2,1)}, u32[]{:S(2)}) copy-start(bf16[768]{0:T(1024)(128)(2,1)} %get-tuple-element.108) | copy-start | bytes 4612
  429.6 7.9 %copy-start.23 = (bf16[768]{0:T(1024)(128)(2,1)S(1)}, bf16[768]{0:T(1024)(128)(2,1)}, u32[]{:S(2)}) copy-start(bf16[768]{0:T(1024)(128)(2,1)} %reduce.10) | copy-start | bytes 4612
  429.6 8.4 %copy-start.16 = (bf16[2304,2,256]{0,2,1:T(8,128)(2,1)S(1)}, bf16[2304,2,256]{0,2,1:T(8,128)(2,1)}, u32[]{:S(2)}) copy-start(bf16[2304,2,256]{0,2,1:T(8,128)(2,1)} %copy.53) | copy-start | bytes 7077892
  473.6 108.6 %copy-start.25 = (f32[2,144]{1,0:T(2,128)S(1)}, f32[2,144]{1,0:T(2,128)}, u32[]{:S(2)}) copy-start(f32[2,144]{1,0:T(2,128)} %param.21) | copy-start | bytes 3460
  473.6 109.9 %copy-start.17 = (f32[2,768,144]{1,2,0:T(8,128)S(1)}, f32[2,768,144]{1,2,0:T(8,128)}, u32[]{:S(2)}) copy-start(f32[2,768,144]{1,2,0:T(8,128)} %param.19) | copy-start | bytes 2654212
  473.6 109.9 %copy-start.18 = (f32[2,768,144]{1,2,0:T(8,128)S(1)}, f32[2,768,144]{1,2,0:T(8,128)}, u32[]{:S(2)}) copy-start(f32[2,768,144]{1,2,0:T(8,128)} %param.18) | copy-start | bytes 2654212
  582.0 6.9 %copy-start.15 = (f32[2,768,144]{1,2,0:T(8,128)S(1)}, f32[2,768,144]{1,2,0:T(8,128)}, u32[]{:S(2)}) copy-start(f32[2,768,144]{1,2,0:T(8,128)} %param.17) | copy-start | bytes 2654212
  582.0 6.9 %copy-start.21 = (f32[2,144]{1,0:T(2,128)S(1)}, f32[2,144]{1,0:T(2,128)}, u32[]{:S(2)}) copy-start(f32[2,144]{1,0:T(2,128)} %compare_select_fusion.2) | copy-start | bytes 3460
  582.2 15.2 %copy-start.26 = (f32[2,144]{1,0:T(2,128)}, f32[2,144]{1,0:T(2,128)S(1)}, u32[]{:S(2)}) copy-start(f32[2,144]{1,0:T(2,128)S(1)} %reshape.252) | copy-start | bytes 3460
  589.0 9.4 %copy-start.13 = (f32[2,768,144]{1,2,0:T(8,128)}, f32[2,768,144]{1,2,0:T(8,128)S(1)}, u32[]{:S(2)}) copy-start(f32[2,768,144]{1,2,0:T(8,128)S(1)} %get-tuple-element.169) | copy-start | bytes 2654212
  589.0 9.4 %copy-start.14 = (f32[2,768,144]{1,2,0:T(8,128)}, f32[2,768,144]{1,2,0:T(8,128)S(1)}, u32[]{:S(2)}) copy-start(f32[2,768,144]{1,2,0:T(8,128)S(1)} %get-tuple-element.168) | copy-start | bytes 2654212
  (6 other events, 8.2 us)
